TPU v7x, 512 devices: a whole 4x8x8 slice. The times are simulated.
512 devices in a mesh: shot: 32 (over z, x), depth: 16 (over y, core).
Axes of the slice: x: 4, y: 8, z: 8, core: 2. Of those that a mesh axis runs over, the one named last changes fastest.
Arguments:
- prev_fields: float32 [32, 2, 128, 64, 128], P('shot', None, 'depth'), may hold values from -6 to 6
- cur_fields: float32 [32, 2, 128, 64, 128], P('shot', None, 'depth'), may hold values from -6 to 6
- speed_term: bfloat16 [32, 128, 64, 128], P('shot', 'depth'), may hold values from 0.039794922 to 0.119628906
- epsilon: bfloat16 [32, 128, 64, 128], P('shot', 'depth'), may hold values from 0 to 0.25
- tilt: bfloat16 [32, 128, 64, 128], P('shot', 'depth'), may hold values from 0 to 1.5
- azimuth: bfloat16 [32, 128, 64, 128], P('shot', 'depth'), may hold values from -3.140625 to 3.140625
- aperture_anchor: int32 [32], replicated, may hold values from -32 to 96
- slot_block: int32 [128], replicated, may hold values from 0 to 127, as said below
- band_width: int32 [128], replicated, may hold values from 1 to 4
- depth_damp: float32 [128], replicated, may hold values from 0.02 to 0.1
Outputs:
- gradient: float32 [128, 128, 128], P('shot', 'depth')
Inputs may be any that keep to these rules, and one draw needn't show every extreme that they name: Slots 4 * q to 4 * q + 3 hold the image blocks 2 r, 2 r + 1, 2 r + 64 and 2 r + 128 / 2 + 1 for some r, each r once, so that slot_block is a permutation of the blocks. `aperture_anchor`: every aperture covers at least 32 image blocks, and at most 2 of them held by one shot index; every aperture reaches 2 for some shot index.
All inputs are finite; a program needn't handle non-finite values.
Results may differ from a plain program's by a relative error of at most 0.0003.
Values may be sent and summed in bfloat16 or wider, within the bound.
No kernel may reach another device: no remote copies, remote signals or barrier semaphores. Data moves between devices by JAX's collectives and lax.ppermute only.
A program may use at most 64 MiB of HBM per device.

v0:
```python
import jax
import jax.numpy as jnp
from jax import lax
from jax.sharding import PartitionSpec as P

NT = 8


def with_halo(cells, sides, width):
    for axis, dim in sides:
        count = lax.axis_size(axis)
        ends = count - 1
        head = lax.slice_in_dim(cells, 0, width, axis=dim)
        tail = lax.slice_in_dim(cells, cells.shape[dim] - width, cells.shape[dim], axis=dim)
        cells = jnp.concatenate(
            [
                lax.ppermute(tail, axis, [(i, (i + 1) % count) for i in range(ends)]),
                cells,
                lax.ppermute(head, axis, [((i + 1) % count, i) for i in range(ends)]),
            ],
            axis=dim,
        )
    return cells


def weights_of(speed_term, epsilon, tilt, azimuth):
    speed = speed_term.astype(jnp.float32)
    ratio = epsilon.astype(jnp.float32)
    theta = tilt.astype(jnp.float32)
    sweep = azimuth.astype(jnp.float32)
    sine = jnp.sin(theta)
    axis_z = jnp.cos(theta)
    axis_x = sine * jnp.cos(sweep)
    axis_y = sine * jnp.sin(sweep)
    iso_part = 1.0 + 2.0 * ratio
    anisotropy = -2.0 * ratio
    return (
        speed * (iso_part + anisotropy * axis_z * axis_z),
        speed * (iso_part + anisotropy * axis_x * axis_x),
        speed * (iso_part + anisotropy * axis_y * axis_y),
        speed * (2.0 * anisotropy * axis_z * axis_x),
        speed * (2.0 * anisotropy * axis_z * axis_y),
        speed * (2.0 * anisotropy * axis_x * axis_y),
    )


def apply_operator(extended, weights):
    leading = extended.ndim - 3
    padded = jnp.pad(extended, [(0, 0)] * leading + [(0, 0), (1, 1), (1, 1)])
    center = padded[..., 1:-1, 1:-1, 1:-1]
    along_z = padded[..., 2:, 1:-1, 1:-1] + padded[..., :-2, 1:-1, 1:-1] - 2.0 * center
    along_x = padded[..., 1:-1, 2:, 1:-1] + padded[..., 1:-1, :-2, 1:-1] - 2.0 * center
    along_y = padded[..., 1:-1, 1:-1, 2:] + padded[..., 1:-1, 1:-1, :-2] - 2.0 * center
    cross_zx = 0.25 * (
        padded[..., 2:, 2:, 1:-1]
        - padded[..., 2:, :-2, 1:-1]
        - padded[..., :-2, 2:, 1:-1]
        + padded[..., :-2, :-2, 1:-1]
    )
    cross_zy = 0.25 * (
        padded[..., 2:, 1:-1, 2:]
        - padded[..., 2:, 1:-1, :-2]
        - padded[..., :-2, 1:-1, 2:]
        + padded[..., :-2, 1:-1, :-2]
    )
    cross_xy = 0.25 * (
        padded[..., 1:-1, 2:, 2:]
        - padded[..., 1:-1, 2:, :-2]
        - padded[..., 1:-1, :-2, 2:]
        + padded[..., 1:-1, :-2, :-2]
    )
    return (
        weights[0] * along_z
        + weights[1] * along_x
        + weights[2] * along_y
        + weights[3] * cross_zx
        + weights[4] * cross_zy
        + weights[5] * cross_xy
    )


def band_matrix(band_width, depth_damp):
    length = band_width.shape[0]
    index = jnp.arange(length, dtype=jnp.int32)
    distance = jnp.abs(index[:, None] - index[None, :])
    reach = jnp.maximum(band_width[:, None], band_width[None, :])
    adjacent = ((distance > 0) & (distance <= reach)).astype(jnp.float32)
    return jnp.diag(depth_damp + jnp.sum(adjacent, axis=1)) - adjacent


def shards(
    prev_fields,
    cur_fields,
    speed_term,
    epsilon,
    tilt,
    azimuth,
    aperture_anchor,
    slot_block,
    band_width,
    depth_damp,
):
    earlier_field = prev_fields[0]
    current = cur_fields[0]
    picture = jnp.zeros(current.shape[1:], jnp.float32)
    weights = weights_of(speed_term[0], epsilon[0], tilt[0], azimuth[0])
    for counter in range(NT):
        extended = with_halo(current, (("depth", 1),), 1)
        following = 2.0 * current - earlier_field + apply_operator(extended, weights)
        picture = picture + following[0] * following[1]
        earlier_field, current = (current, following)
    picture = picture * (1.0 / NT)
    shots = lax.axis_size("shot")
    my_shot = lax.axis_index("shot")
    span = picture.shape[1]
    offsets = jnp.arange(span, dtype=jnp.int32)
    target = aperture_anchor[:, None] + offsets[None, :]
    matches = slot_block[None, None, :] == target[:, :, None]
    shot_ids = jnp.arange(shots, dtype=jnp.int32)
    mine = shot_ids == my_shot
    selector = jnp.any(matches & mine[:, None, None], axis=0).astype(jnp.float32)
    owned = lax.psum_scatter(
        jnp.einsum("kp,zky->pyz", selector, picture, precision=lax.Precision.HIGHEST),
        "shot",
        scatter_dimension=0,
        tiled=True,
    )
    traces = lax.all_to_all(owned, "depth", split_axis=1, concat_axis=2, tiled=True)
    depth_total = traces.shape[2]
    columns = traces.reshape(-1, depth_total)
    matrix = band_matrix(band_width, depth_damp)
    factor = jnp.linalg.cholesky(matrix)
    solved = jax.scipy.linalg.cho_solve((factor, True), columns.T)
    return solved.T.reshape(traces.shape)


def solution(mesh):
    placed = (
        P("shot", None, "depth", None, None),
        P("shot", None, "depth", None, None),
        P("shot", "depth", None, None),
        P("shot", "depth", None, None),
        P("shot", "depth", None, None),
        P("shot", "depth", None, None),
        P(),
        P(),
        P(),
        P(),
    )
    return jax.shard_map(
        shards, mesh=mesh, in_specs=placed, out_specs=P("shot", "depth", None), check_vma=False
    )
```

profile of v0, /device:TPU:1, one launch (start us, length us, event | category | flops | bytes accessed | tf_op | source)
XLA Modules:
  0.0 357.2 jit_solution(3258238092397935642)
XLA Ops:
  6.5 0.9 fusion.194
  7.5 8.7 %collective-permute-start = (f32[2,1,64,128]{3,2,1,0:T(8,128)S(1)}, f32[2,1,64,128]{3,2,1,0:T(8,128)S(1)}, u32[]{:S(2)}, u32[]{:S(2)}) collective-permute-start(f32[2,1,64,128]{3,2,1,0:T(8,128)S(1)} %get-tuple-element.25), channel_id=1, source_target_pairs={{1,0},{2,1},{3,2},{4,3},{5,4},{6,5},{7,6},{8,7},{9,8},{10,9},{11,1... | collective-permute-start | bytes 196616 | tf_op jit(solution)/shard_map/ppermute | solution.py:19
  16.2 1.9 collective-permute-start.1
  18.2 3.3 fusion.141
  22.0 0.5 copy-done.5
  22.5 1.6 fusion.117
  24.2 2.4 collective-permute-start.2
  26.6 3.2 collective-permute-start.3
  29.7 1.3 collective-permute-done.3
  31.5 1.6 fusion.101
  33.2 1.9 collective-permute-start.4
  35.1 4.3 %collective-permute-start.5 = (f32[2,1,64,128]{3,2,1,0:T(8,128)S(1)}, f32[2,1,64,128]{3,2,1,0:T(8,128)S(1)}, u32[]{:S(2)}, u32[]{:S(2)}) collective-permute-start(f32[2,1,64,128]{3,2,1,0:T(8,128)S(1)} %get-tuple-element.15), channel_id=1, source_target_pairs={{0,1},{1,2},{2,3},{3,4},{4,5},{5,6},{6,7},{7,8},{8,9},{9,10},{10,1... | collective-permute-start | bytes 196616 | tf_op jit(solution)/shard_map/ppermute | solution.py:17
  39.4 1.3 collective-permute-done.5
  41.1 1.6 fusion.85
  42.8 1.9 collective-permute-start.6
  44.7 4.3 %collective-permute-start.7 = (f32[2,1,64,128]{3,2,1,0:T(8,128)S(1)}, f32[2,1,64,128]{3,2,1,0:T(8,128)S(1)}, u32[]{:S(2)}, u32[]{:S(2)}) collective-permute-start(f32[2,1,64,128]{3,2,1,0:T(8,128)S(1)} %get-tuple-element.13), channel_id=1, source_target_pairs={{0,1},{1,2},{2,3},{3,4},{4,5},{5,6},{6,7},{7,8},{8,9},{9,10},{10,1... | collective-permute-start | bytes 196616 | tf_op jit(solution)/shard_map/ppermute | solution.py:17
  49.0 1.3 collective-permute-done.7
  50.8 1.6 fusion.69
  52.4 1.9 collective-permute-start.8
  54.4 4.4 %collective-permute-start.9 = (f32[2,1,64,128]{3,2,1,0:T(8,128)S(1)}, f32[2,1,64,128]{3,2,1,0:T(8,128)S(1)}, u32[]{:S(2)}, u32[]{:S(2)}) collective-permute-start(f32[2,1,64,128]{3,2,1,0:T(8,128)S(1)} %get-tuple-element.11), channel_id=1, source_target_pairs={{0,1},{1,2},{2,3},{3,4},{4,5},{5,6},{6,7},{7,8},{8,9},{9,10},{10,1... | collective-permute-start | bytes 196616 | tf_op jit(solution)/shard_map/ppermute | solution.py:17
  58.8 1.1 collective-permute-done.9
  60.4 1.6 fusion.53
  62.1 0.8 copy-done.2
  62.9 1.9 collective-permute-start.10
  64.8 4.3 %collective-permute-start.11 = (f32[2,1,64,128]{3,2,1,0:T(8,128)S(1)}, f32[2,1,64,128]{3,2,1,0:T(8,128)S(1)}, u32[]{:S(2)}, u32[]{:S(2)}) collective-permute-start(f32[2,1,64,128]{3,2,1,0:T(8,128)S(1)} %get-tuple-element.9), channel_id=1, source_target_pairs={{0,1},{1,2},{2,3},{3,4},{4,5},{5,6},{6,7},{7,8},{8,9},{9,10},{10,1... | collective-permute-start | bytes 196616 | tf_op jit(solution)/shard_map/ppermute | solution.py:17
  69.2 1.2 collective-permute-done.11
  70.4 1.5 select_maximum_fusion.4
  71.9 1.6 fusion.37
  73.5 1.9 collective-permute-start.12
  75.5 4.3 %collective-permute-start.13 = (f32[2,1,64,128]{3,2,1,0:T(8,128)S(1)}, f32[2,1,64,128]{3,2,1,0:T(8,128)S(1)}, u32[]{:S(2)}, u32[]{:S(2)}) collective-permute-start(f32[2,1,64,128]{3,2,1,0:T(8,128)S(1)} %get-tuple-element.7), channel_id=1, source_target_pairs={{0,1},{1,2},{2,3},{3,4},{4,5},{5,6},{6,7},{7,8},{8,9},{9,10},{10,1... | collective-permute-start | bytes 196616 | tf_op jit(solution)/shard_map/ppermute | solution.py:17
  79.8 1.3 collective-permute-done.13
  81.5 1.6 fusion.21
  83.2 1.9 collective-permute-start.14
  85.1 4.5 %collective-permute-start.15 = (f32[2,1,64,128]{3,2,1,0:T(8,128)S(1)}, f32[2,1,64,128]{3,2,1,0:T(8,128)S(1)}, u32[]{:S(2)}, u32[]{:S(2)}) collective-permute-start(f32[2,1,64,128]{3,2,1,0:T(8,128)S(1)} %get-tuple-element.5), channel_id=1, source_target_pairs={{0,1},{1,2},{2,3},{3,4},{4,5},{5,6},{6,7},{7,8},{8,9},{9,10},{10,1... | collective-permute-start | bytes 196616 | tf_op jit(solution)/shard_map/ppermute | solution.py:17
  90.1 0.6 collective-permute-done.15
  91.1 1.6 fusion.5
  92.8 0.8 convolution_bitcast_fusion
  93.7 1.0 copy.19
  95.0 11.7 %cholesky.16 = f32[128,128]{1,0:T(8,128)S(1)} custom-call(f32[128,128]{1,0:T(8,128)S(1)} %fusion.176), custom_call_target="Cholesky" | custom-call | tf_op jit(solution)/shard_map/jit(cholesky)/cholesky | solution.py:132
  106.8 0.7 compare_reduce_fusion
  107.4 215.2 %reduce-scatter.2.cloned.1.call-done = f32[4,128,8]{1,2,0:T(8,128)} async-done(((f32[128,128,8]{1,2,0:T(8,128)}), f32[4,128,8]{1,2,0:T(8,128)}) %reduce-scatter.2.cloned.1.call-update) | async-done | bytes 16400 | tf_op jit(solution)/shard_map/reduce_scatter | solution.py:122
  322.6 0.9 copy.20
  323.4 0.9 reshape.74
  324.3 12.8 %all-to-all-start = ((f32[16,1,256]{2,1,0:T(1,128)}), f32[16,1,256]{2,1,0:T(1,128)S(1)}, u32[]{:S(2)}, u32[]{:S(2)}) async-start(f32[16,1,256]{2,1,0:T(1,128)} %reshape.74), calls=%async_computation.1 | async-start | bytes 32768 | tf_op jit(solution)/shard_map/all_to_all | solution.py:128
  337.1 0.6 fusion.174
  337.7 9.8 %custom-call.10 = f32[1,128,128]{1,2,0:T(8,128)S(1)} custom-call(f32[1,128,128]{2,1,0:T(8,128)S(1)} %fusion.174), custom_call_target="InvertDiagBlocksLowerTriangular" | custom-call | tf_op jit(solution)/shard_map/jit(_cho_solve)/triangular_solve | solution.py:133
  348.0 0.7 reduce.6
  349.6 0.8 fusion.177
  (56 shorter events, 5.5 us)
Async XLA Ops:
  6.5 15.0 %copy-start.4 = (f32[1,2,8,64,128]{4,3,2,1,0:T(8,128)S(1)}, f32[1,2,8,64,128]{4,3,2,1,0:T(8,128)}, u32[]{:S(2)}) copy-start(f32[1,2,8,64,128]{4,3,2,1,0:T(8,128)} %param.11) | copy-start | bytes 1572868
  6.5 316.0 %reduce-scatter.2.cloned.1.call-start = ((), (), s32[]{:S(2)}) async-start(), calls=%async_computation.2 | async-start | bytes 540672 | tf_op jit(solution)/shard_map/reduce_scatter | solution.py:122
  7.5 14.0 %collective-permute-start = (f32[2,1,64,128]{3,2,1,0:T(8,128)S(1)}, f32[2,1,64,128]{3,2,1,0:T(8,128)S(1)}, u32[]{:S(2)}, u32[]{:S(2)}) collective-permute-start(f32[2,1,64,128]{3,2,1,0:T(8,128)S(1)} %get-tuple-element.25), channel_id=1, source_target_pairs={{1,0},{2,1},{3,2},{4,3},{5,4},{6,5},{7,6},{8,7},{9,8},{10,9},{11,1... | collective-permute-start | bytes 196616 | tf_op jit(solution)/shard_map/ppermute | solution.py:19
  16.2 5.2 %collective-permute-start.1 = (f32[2,1,64,128]{3,2,1,0:T(8,128)S(1)}, f32[2,1,64,128]{3,2,1,0:T(8,128)S(1)}, u32[]{:S(2)}, u32[]{:S(2)}) collective-permute-start(f32[2,1,64,128]{3,2,1,0:T(8,128)S(1)} %get-tuple-element.24), channel_id=1, source_target_pairs={{0,1},{1,2},{2,3},{3,4},{4,5},{5,6},{6,7},{7,8},{8,9},{9,10},{10,1... | collective-permute-start | bytes 196616 | tf_op jit(solution)/shard_map/ppermute | solution.py:17
  21.5 1.0 copy-start.5
  24.2 5.6 %collective-permute-start.2 = (f32[2,1,64,128]{3,2,1,0:T(8,128)S(1)}, f32[2,1,64,128]{3,2,1,0:T(8,128)S(1)}, u32[]{:S(2)}, u32[]{:S(2)}) collective-permute-start(f32[2,1,64,128]{3,2,1,0:T(8,128)S(1)} %get-tuple-element.18), channel_id=1, source_target_pairs={{1,0},{2,1},{3,2},{4,3},{5,4},{6,5},{7,6},{8,7},{9,8},{10,9},{11,1... | collective-permute-start | bytes 196616 | tf_op jit(solution)/shard_map/ppermute | solution.py:19
  26.6 4.5 %collective-permute-start.3 = (f32[2,1,64,128]{3,2,1,0:T(8,128)S(1)}, f32[2,1,64,128]{3,2,1,0:T(8,128)S(1)}, u32[]{:S(2)}, u32[]{:S(2)}) collective-permute-start(f32[2,1,64,128]{3,2,1,0:T(8,128)S(1)} %get-tuple-element.17), channel_id=1, source_target_pairs={{0,1},{1,2},{2,3},{3,4},{4,5},{5,6},{6,7},{7,8},{8,9},{9,10},{10,1... | collective-permute-start | bytes 196616 | tf_op jit(solution)/shard_map/ppermute | solution.py:17
  33.2 6.2 %collective-permute-start.4 = (f32[2,1,64,128]{3,2,1,0:T(8,128)S(1)}, f32[2,1,64,128]{3,2,1,0:T(8,128)S(1)}, u32[]{:S(2)}, u32[]{:S(2)}) collective-permute-start(f32[2,1,64,128]{3,2,1,0:T(8,128)S(1)} %get-tuple-element.16), channel_id=1, source_target_pairs={{1,0},{2,1},{3,2},{4,3},{5,4},{6,5},{7,6},{8,7},{9,8},{10,9},{11,1... | collective-permute-start | bytes 196616 | tf_op jit(solution)/shard_map/ppermute | solution.py:19
  35.1 5.6 %collective-permute-start.5 = (f32[2,1,64,128]{3,2,1,0:T(8,128)S(1)}, f32[2,1,64,128]{3,2,1,0:T(8,128)S(1)}, u32[]{:S(2)}, u32[]{:S(2)}) collective-permute-start(f32[2,1,64,128]{3,2,1,0:T(8,128)S(1)} %get-tuple-element.15), channel_id=1, source_target_pairs={{0,1},{1,2},{2,3},{3,4},{4,5},{5,6},{6,7},{7,8},{8,9},{9,10},{10,1... | collective-permute-start | bytes 196616 | tf_op jit(solution)/shard_map/ppermute | solution.py:17
  42.8 6.2 %collective-permute-start.6 = (f32[2,1,64,128]{3,2,1,0:T(8,128)S(1)}, f32[2,1,64,128]{3,2,1,0:T(8,128)S(1)}, u32[]{:S(2)}, u32[]{:S(2)}) collective-permute-start(f32[2,1,64,128]{3,2,1,0:T(8,128)S(1)} %get-tuple-element.14), channel_id=1, source_target_pairs={{1,0},{2,1},{3,2},{4,3},{5,4},{6,5},{7,6},{8,7},{9,8},{10,9},{11,1... | collective-permute-start | bytes 196616 | tf_op jit(solution)/shard_map/ppermute | solution.py:19
  44.7 5.6 %collective-permute-start.7 = (f32[2,1,64,128]{3,2,1,0:T(8,128)S(1)}, f32[2,1,64,128]{3,2,1,0:T(8,128)S(1)}, u32[]{:S(2)}, u32[]{:S(2)}) collective-permute-start(f32[2,1,64,128]{3,2,1,0:T(8,128)S(1)} %get-tuple-element.13), channel_id=1, source_target_pairs={{0,1},{1,2},{2,3},{3,4},{4,5},{5,6},{6,7},{7,8},{8,9},{9,10},{10,1... | collective-permute-start | bytes 196616 | tf_op jit(solution)/shard_map/ppermute | solution.py:17
  52.4 9.6 %copy-start = (f32[2,8,64,128]{3,2,1,0:T(8,128)}, f32[2,8,64,128]{3,2,1,0:T(8,128)S(1)}, u32[]{:S(2)}) copy-start(f32[2,8,64,128]{3,2,1,0:T(8,128)S(1)} %fusion.69) | copy-start | bytes 1572868
  52.4 6.4 %collective-permute-start.8 = (f32[2,1,64,128]{3,2,1,0:T(8,128)S(1)}, f32[2,1,64,128]{3,2,1,0:T(8,128)S(1)}, u32[]{:S(2)}, u32[]{:S(2)}) collective-permute-start(f32[2,1,64,128]{3,2,1,0:T(8,128)S(1)} %get-tuple-element.12), channel_id=1, source_target_pairs={{1,0},{2,1},{3,2},{4,3},{5,4},{6,5},{7,6},{8,7},{9,8},{10,9},{11,1... | collective-permute-start | bytes 196616 | tf_op jit(solution)/shard_map/ppermute | solution.py:19
  54.4 5.6 %collective-permute-start.9 = (f32[2,1,64,128]{3,2,1,0:T(8,128)S(1)}, f32[2,1,64,128]{3,2,1,0:T(8,128)S(1)}, u32[]{:S(2)}, u32[]{:S(2)}) collective-permute-start(f32[2,1,64,128]{3,2,1,0:T(8,128)S(1)} %get-tuple-element.11), channel_id=1, source_target_pairs={{0,1},{1,2},{2,3},{3,4},{4,5},{5,6},{6,7},{7,8},{8,9},{9,10},{10,1... | collective-permute-start | bytes 196616 | tf_op jit(solution)/shard_map/ppermute | solution.py:17
  60.4 8.7 %copy-start.7 = (s32[32]{0:T(128)S(1)}, s32[32]{0:T(128)}, u32[]{:S(2)}) copy-start(s32[32]{0:T(128)} %param.16) | copy-start | bytes 388
  62.1 0.8 copy-start.2
  62.9 6.3 %collective-permute-start.10 = (f32[2,1,64,128]{3,2,1,0:T(8,128)S(1)}, f32[2,1,64,128]{3,2,1,0:T(8,128)S(1)}, u32[]{:S(2)}, u32[]{:S(2)}) collective-permute-start(f32[2,1,64,128]{3,2,1,0:T(8,128)S(1)} %get-tuple-element.10), channel_id=1, source_target_pairs={{1,0},{2,1},{3,2},{4,3},{5,4},{6,5},{7,6},{8,7},{9,8},{10,9},{11,1... | collective-permute-start | bytes 196616 | tf_op jit(solution)/shard_map/ppermute | solution.py:19
  64.8 5.6 %collective-permute-start.11 = (f32[2,1,64,128]{3,2,1,0:T(8,128)S(1)}, f32[2,1,64,128]{3,2,1,0:T(8,128)S(1)}, u32[]{:S(2)}, u32[]{:S(2)}) collective-permute-start(f32[2,1,64,128]{3,2,1,0:T(8,128)S(1)} %get-tuple-element.9), channel_id=1, source_target_pairs={{0,1},{1,2},{2,3},{3,4},{4,5},{5,6},{6,7},{7,8},{8,9},{9,10},{10,1... | collective-permute-start | bytes 196616 | tf_op jit(solution)/shard_map/ppermute | solution.py:17
  69.2 2.7 copy-start.1
  69.2 2.7 copy-start.3
  73.5 6.2 %collective-permute-start.12 = (f32[2,1,64,128]{3,2,1,0:T(8,128)S(1)}, f32[2,1,64,128]{3,2,1,0:T(8,128)S(1)}, u32[]{:S(2)}, u32[]{:S(2)}) collective-permute-start(f32[2,1,64,128]{3,2,1,0:T(8,128)S(1)} %get-tuple-element.8), channel_id=1, source_target_pairs={{1,0},{2,1},{3,2},{4,3},{5,4},{6,5},{7,6},{8,7},{9,8},{10,9},{11,1... | collective-permute-start | bytes 196616 | tf_op jit(solution)/shard_map/ppermute | solution.py:19
  75.5 5.6 %collective-permute-start.13 = (f32[2,1,64,128]{3,2,1,0:T(8,128)S(1)}, f32[2,1,64,128]{3,2,1,0:T(8,128)S(1)}, u32[]{:S(2)}, u32[]{:S(2)}) collective-permute-start(f32[2,1,64,128]{3,2,1,0:T(8,128)S(1)} %get-tuple-element.7), channel_id=1, source_target_pairs={{0,1},{1,2},{2,3},{3,4},{4,5},{5,6},{6,7},{7,8},{8,9},{9,10},{10,1... | collective-permute-start | bytes 196616 | tf_op jit(solution)/shard_map/ppermute | solution.py:17
  81.5 8.1 %copy-start.8 = (s32[128]{0:T(128)S(1)}, s32[128]{0:T(128)}, u32[]{:S(2)}) copy-start(s32[128]{0:T(128)} %param.17) | copy-start | bytes 1540
  83.2 6.9 %collective-permute-start.14 = (f32[2,1,64,128]{3,2,1,0:T(8,128)S(1)}, f32[2,1,64,128]{3,2,1,0:T(8,128)S(1)}, u32[]{:S(2)}, u32[]{:S(2)}) collective-permute-start(f32[2,1,64,128]{3,2,1,0:T(8,128)S(1)} %get-tuple-element.6), channel_id=1, source_target_pairs={{1,0},{2,1},{3,2},{4,3},{5,4},{6,5},{7,6},{8,7},{9,8},{10,9},{11,1... | collective-permute-start | bytes 196616 | tf_op jit(solution)/shard_map/ppermute | solution.py:19
  85.1 5.6 %collective-permute-start.15 = (f32[2,1,64,128]{3,2,1,0:T(8,128)S(1)}, f32[2,1,64,128]{3,2,1,0:T(8,128)S(1)}, u32[]{:S(2)}, u32[]{:S(2)}) collective-permute-start(f32[2,1,64,128]{3,2,1,0:T(8,128)S(1)} %get-tuple-element.5), channel_id=1, source_target_pairs={{0,1},{1,2},{2,3},{3,4},{4,5},{5,6},{6,7},{7,8},{8,9},{9,10},{10,1... | collective-permute-start | bytes 196616 | tf_op jit(solution)/shard_map/ppermute | solution.py:17
  92.8 1.9 copy-start.6
  92.8 2.1 copy-start.9
  324.3 23.2 %all-to-all-start = ((f32[16,1,256]{2,1,0:T(1,128)}), f32[16,1,256]{2,1,0:T(1,128)S(1)}, u32[]{:S(2)}, u32[]{:S(2)}) async-start(f32[16,1,256]{2,1,0:T(1,128)} %reshape.74), calls=%async_computation.1 | async-start | bytes 32768 | tf_op jit(solution)/shard_map/all_to_all | solution.py:128
Sparse Core Ops, SparseCore 0:
  94.8 227.7 reduce-scatter.1
where the time goes:
time: 358 us; the launch traced here: 357 us
  waiting for transfers between devices  223 us (62%)
  starting transfers between devices  66.5 us (19%)
  other arithmetic  45.4 us (13%)
  between operations  14 us (4%)
  local copies, waits for them, and re-layouts  6.28 us (2%)
    reduce_scatter x1, waiting for transfers between devices, shards(): lax.psum_scatter(jnp.einsum('kp,zky->pyz', selector, picture, precision=l...  215 us
    ppermute x8, starting transfers between devices, with_halo(): lax.ppermute(tail, axis, [(i, (i + 1) % count) for i in range(ends)])  31.1 us
    ppermute x8, starting transfers between devices, with_halo(): lax.ppermute(head, axis, [((i + 1) % count, i) for i in range(ends)])  22.7 us
    add x8, other arithmetic, shards(): 2.0 * current - earlier_field + apply_operator(extended, weights)  13.1 us
    all_to_all x1, starting transfers between devices, shards(): lax.all_to_all(owned, 'depth', split_axis=1, concat_axis=2, tiled=True)  12.8 us
    another operation x3, other arithmetic, shards(): factor = jnp.linalg.cholesky(matrix)  12.4 us
    another operation x2, other arithmetic, shards(): solved = jax.scipy.linalg.cho_solve((factor, True), columns.T)  10.4 us
    ppermute x8, waiting for transfers between devices, with_halo(): lax.ppermute(tail, axis, [(i, (i + 1) % count) for i in range(ends)])  8.08 us
  transfers between devices with their start and end apart: 18, of which 8 were waited for; matrix products, arithmetic and copies ran while one was open for 8% of the time, Pallas kernels for 0%

commit v1 on v0

v1 whole, which is shorter than its diff:
```python
import jax
import jax.numpy as jnp
from jax import lax
from jax.experimental import pallas as pl
from jax.experimental.pallas import tpu as pltpu
from jax.sharding import PartitionSpec as P

NT = 8
W = 8
SLAB = 8
EXT = SLAB + 2 * W
AX = 64
AY = 128
PAD = 8


def trig(angle):
    square = angle * angle
    sine = -1.0 / 39916800.0
    for term in (1.0 / 362880.0, -1.0 / 5040.0, 1.0 / 120.0, -1.0 / 6.0, 1.0):
        sine = sine * square + term
    cosine = 1.0 / 479001600.0
    for term in (-1.0 / 3628800.0, 1.0 / 40320.0, -1.0 / 720.0, 1.0 / 24.0, -0.5, 1.0):
        cosine = cosine * square + term
    return sine * angle, cosine


def weight_planes(speed, ratio, theta, sweep):
    sine, axis_z = trig(theta)
    half_sine, half_cosine = trig(0.5 * sweep)
    axis_x = sine * (1.0 - 2.0 * half_sine * half_sine)
    axis_y = sine * (2.0 * half_sine * half_cosine)
    tilted = -2.0 * ratio
    base = speed * (1.0 + 2.0 * ratio)
    tilted = speed * tilted
    cross = 0.5 * tilted
    zz = base + tilted * axis_z * axis_z
    xx = base + tilted * axis_x * axis_x
    yy = base + tilted * axis_y * axis_y
    zx = cross * axis_z * axis_x
    zy = cross * axis_z * axis_y
    xy = cross * axis_x * axis_y
    centre = 2.0 - 2.0 * (zz + xx + yy)
    lane = lax.broadcasted_iota(jnp.int32, speed.shape, 1)
    low = lane == 0
    high = lane == AY - 1

    def up(plane):
        return jnp.where(high, 0.0, pltpu.roll(plane, AY - 1, 1))

    def down(plane):
        return jnp.where(low, 0.0, pltpu.roll(plane, 1, 1))

    return (centre, zz, xx, zx, up(yy), up(-zy), up(-xy), down(yy), down(zy), down(xy))


def stencil_kernel(
    edge, source, cur, prev, speed, ratio, tilt, azimuth,
    cur_low, prev_low, media_low, cur_high, prev_high, media_high,
    send, first, second, planes, picture, *, rows=16, unroll=1,
):
    low_scale = edge[0]
    high_scale = edge[1]
    zeros = jnp.zeros((PAD, AY), jnp.float32)

    body = pl.ds(PAD, AX)
    for field in range(2):
        def clear(layer, carry):
            for buffer in (first, second):
                buffer[field, layer, 0:PAD, :] = zeros
                buffer[field, layer, PAD + AX : PAD + AX + PAD, :] = zeros
            return carry
        lax.fori_loop(0, EXT, clear, 0)

        def load(layer, carry):
            first[field, layer, body, :] = cur_low[field, layer] * low_scale
            first[field, layer + W, body, :] = cur[field, layer]
            first[field, layer + W + SLAB, body, :] = cur_high[field, layer] * high_scale
            second[field, layer + W, body, :] = prev[field, layer]
            return carry
        lax.fori_loop(0, SLAB, load, 0)

        def load_prev(layer, carry):
            second[field, layer + 1, body, :] = prev_low[field, layer] * low_scale
            second[field, layer + W + SLAB, body, :] = prev_high[field, layer] * high_scale
            return carry
        lax.fori_loop(0, W - 1, load_prev, 0)

    def store_planes(layer, speed_part, ratio_part, tilt_part, azimuth_part, scale):
        for start in range(0, AX, 16):
            part = slice(start, start + 16)
            values = weight_planes(
                speed_part[part].astype(jnp.float32) * scale,
                ratio_part[part].astype(jnp.float32),
                tilt_part[part].astype(jnp.float32),
                azimuth_part[part].astype(jnp.float32),
            )
            for index, value in enumerate(values):
                planes[index, layer, part, :] = value

    def own_planes(layer, carry):
        store_planes(layer + W - 1, speed.at[layer], ratio.at[layer], tilt.at[layer], azimuth.at[layer], 1.0)
        return carry

    lax.fori_loop(0, SLAB, own_planes, 0)

    def halo_planes(layer, carry):
        store_planes(layer, *[media_low.at[i, layer] for i in range(4)], low_scale)
        store_planes(layer + W - 1 + SLAB, *[media_high.at[i, layer] for i in range(4)], high_scale)
        return carry

    lax.fori_loop(0, W - 1, halo_planes, 0)

    def advance(source_buffer, target, layer, start):
        part = slice(start, start + rows)
        (centre_w, zz, xx, zx, y_low, zy_low, xy_low, y_high, zy_high, xy_high) = [
            planes[i, layer - 1, part, :] for i in range(10)
        ]
        here = slice(PAD + start, PAD + start + rows)
        before = slice(PAD + start - 1, PAD + start + rows - 1)
        after = slice(PAD + start + 1, PAD + start + rows + 1)
        made = []
        for field in range(2):
            centre = source_buffer[field, layer, here, :]
            above = source_buffer[field, layer + 1, here, :]
            below = source_buffer[field, layer - 1, here, :]
            ahead = source_buffer[field, layer, after, :]
            behind = source_buffer[field, layer, before, :]
            step_z = above - below
            step_x = ahead - behind
            twist = (source_buffer[field, layer + 1, after, :] - source_buffer[field, layer + 1, before, :]) - (
                source_buffer[field, layer - 1, after, :] - source_buffer[field, layer - 1, before, :]
            )
            total = centre_w * centre - target[field, layer, here, :]
            total = total + zz * (above + below)
            total = total + xx * (ahead + behind)
            total = total + zx * twist
            total = total + pltpu.roll(y_low * centre + zy_low * step_z + xy_low * step_x, 1, 1)
            total = total + pltpu.roll(y_high * centre + zy_high * step_z + xy_high * step_x, AY - 1, 1)
            target[field, layer, here, :] = total
            made.append(total)
        return made

    for step in range(1, NT + 1):
        source_buffer, target = (first, second) if step % 2 else (second, first)

        def halo(layer, carry):
            for start in range(0, AX, rows):
                advance(source_buffer, target, layer, start)
            return carry

        def own(layer, carry):
            for start in range(0, AX, rows):
                made = advance(source_buffer, target, layer + W, start)
                place = pl.ds(pl.multiple_of(layer * AX + start, rows), rows)
                product = made[0] * made[1]
                picture[place, :] = product if step == 1 else picture[place, :] + product
            return carry

        if step < NT:
            lax.fori_loop(step, W, halo, 0, unroll=unroll)
        lax.fori_loop(0, SLAB, own, 0, unroll=unroll)
        if step < NT:
            lax.fori_loop(W + SLAB, EXT - step, halo, 0, unroll=unroll)

    for entry in range(source.shape[0]):
        send[entry] = picture[pl.ds(source[entry], SLAB, stride=AX), :]


def stencil(edge, source, cur, prev, speed, ratio, tilt, azimuth, lows, highs):
    vm = pl.BlockSpec(memory_space=pltpu.VMEM)
    sm = pl.BlockSpec(memory_space=pltpu.SMEM)
    n = source.shape[0]
    return pl.pallas_call(
        stencil_kernel,
        out_shape=jax.ShapeDtypeStruct((n, SLAB, AY), jnp.float32),
        in_specs=[sm, sm] + [vm] * 12,
        out_specs=vm,
        scratch_shapes=[
            pltpu.VMEM((2, EXT, AX + 2 * PAD, AY), jnp.float32),
            pltpu.VMEM((2, EXT, AX + 2 * PAD, AY), jnp.float32),
            pltpu.VMEM((10, EXT - 2, AX, AY), jnp.float32),
            pltpu.VMEM((SLAB * AX, AY), jnp.float32),
        ],
    )(edge, source, cur, prev, speed, ratio, tilt, azimuth, *lows, *highs)


VM = pl.BlockSpec(memory_space=pltpu.VMEM)
SM = pl.BlockSpec(memory_space=pltpu.SMEM)
DOUBLINGS = 14


def inverse_kernel(jump, column_scale, inverse, stack):
    size = jump.shape[0]
    row = lax.broadcasted_iota(jnp.int32, (size, size), 0)
    column = lax.broadcasted_iota(jnp.int32, (size, size), 1)
    stack[0:size, :] = (row == column).astype(jnp.float32)
    stack[size : 2 * size, :] = jump[...]

    def double(counter, carry):
        grown = lax.dot_general(
            stack[...], stack[size : 2 * size, :], (((1,), (0,)), ((), ())),
            precision=lax.Precision.HIGHEST, preferred_element_type=jnp.float32,
        )
        stack[0:size, :] = stack[0:size, :] + grown[:size]
        stack[size : 2 * size, :] = grown[size:]
        return carry

    lax.fori_loop(0, DOUBLINGS, double, 0)
    inverse[...] = stack[0:size, :] * column_scale[...]


def band_inverse(band_width, depth_damp):
    length = band_width.shape[0]
    index = jnp.arange(length, dtype=jnp.int32)
    distance = jnp.abs(index[:, None] - index[None, :])
    reach = jnp.maximum(band_width[:, None], band_width[None, :])
    adjacent = ((distance > 0) & (distance <= reach)).astype(jnp.float32)
    diagonal = depth_damp + jnp.sum(adjacent, axis=1)
    scale = 1.0 / diagonal
    return pl.pallas_call(
        inverse_kernel,
        out_shape=jax.ShapeDtypeStruct((length, length), jnp.float32),
        in_specs=[VM, VM],
        out_specs=VM,
        scratch_shapes=[pltpu.VMEM((2 * length, length), jnp.float32)],
    )(adjacent * scale[:, None], scale[None, :])


def gather_kernel(place, rows_in, out, held):
    for slot in range(held.shape[0]):
        held[slot] = jnp.zeros((SLAB, AY), jnp.float32)
    for entry in range(rows_in.shape[0]):
        slot = place[entry]
        held[slot] = held[slot] + rows_in[entry]
    slots = held.shape[0] - 1
    part = AY // out.shape[0]
    lane = lax.broadcasted_iota(jnp.int32, (SLAB, AY), 1)
    for piece in range(out.shape[0]):
        mixed = None
        for slot in range(slots):
            moved = held[slot]
            turn = (slot * part - piece * part) % AY
            if turn:
                moved = pltpu.roll(moved, turn, 1)
            mixed = moved if mixed is None else jnp.where(lane >= slot * part, moved, mixed)
        out[piece] = mixed * (1.0 / NT)


def apply_kernel(inverse, columns, out):
    solved = lax.dot_general(
        columns[...], inverse[...], (((0,), (1,)), ((), ())),
        precision=lax.Precision.HIGHEST, preferred_element_type=jnp.float32,
    )
    slots, part = out.shape[:2]
    for slot in range(slots):
        out[slot] = solved[slot * part : (slot + 1) * part]


def pick_rows(blocks, anchors):
    row = blocks - anchors
    valid = (row >= 0) & (row < AX)
    order = jnp.cumsum(valid.astype(jnp.int32), axis=1) - 1
    return row, valid, order


def shards(
    prev_fields, cur_fields, speed_term, epsilon, tilt, azimuth,
    aperture_anchor, slot_block, band_width, depth_damp,
):
    depth = lax.axis_size("depth")
    shots = lax.axis_size("shot")
    upward = [(i, (i + 1) % depth) for i in range(depth)]
    downward = [((i + 1) % depth, i) for i in range(depth)]
    prev, cur = prev_fields[0], cur_fields[0]
    media = [speed_term[0], epsilon[0], tilt[0], azimuth[0]]
    media_tail = jnp.stack([part[1:] for part in media])
    media_head = jnp.stack([part[: W - 1] for part in media])
    cur_low = lax.ppermute(cur, "depth", upward)
    cur_high = lax.ppermute(cur, "depth", downward)
    lows = (cur_low, lax.ppermute(prev[:, 1:], "depth", upward), lax.ppermute(media_tail, "depth", upward))
    highs = (
        cur_high,
        lax.ppermute(prev[:, : W - 1], "depth", downward),
        lax.ppermute(media_head, "depth", downward),
    )
    my_depth = lax.axis_index("depth")
    my_shot = lax.axis_index("shot")
    edge = jnp.stack([my_depth > 0, my_depth < depth - 1]).astype(jnp.float32)

    held = slot_block.shape[0] // shots
    blocks = slot_block.reshape(shots, held)
    row, valid, order = pick_rows(blocks, aperture_anchor[my_shot])
    source = jnp.stack(
        [jnp.sum(jnp.where(valid & (order == j), row, 0), axis=1) for j in range(2)], axis=1
    ).reshape(-1)
    mine = lax.dynamic_slice_in_dim(slot_block, my_shot * held, held)
    row, valid, order = pick_rows(mine[None, :], aperture_anchor[:, None])
    slot = jnp.arange(held, dtype=jnp.int32)[None, :]
    place = jnp.stack(
        [held + jnp.sum(jnp.where(valid & (order == j), slot - held, 0), axis=1) for j in range(2)], axis=1
    ).reshape(-1)
    inverse = band_inverse(band_width, depth_damp)

    send = stencil(edge, source, cur, prev, *media, lows, highs)
    received = lax.all_to_all(send, "shot", split_axis=0, concat_axis=0, tiled=True)
    part = AY // depth
    pieces = pl.pallas_call(
        gather_kernel,
        out_shape=jax.ShapeDtypeStruct((depth, SLAB, AY), jnp.float32),
        in_specs=[SM, VM],
        out_specs=VM,
        scratch_shapes=[pltpu.VMEM((held + 1, SLAB, AY), jnp.float32)],
    )(place, received)
    columns = lax.all_to_all(pieces, "depth", split_axis=0, concat_axis=0, tiled=True)
    return pl.pallas_call(
        apply_kernel,
        out_shape=jax.ShapeDtypeStruct((held, part, AY), jnp.float32),
        in_specs=[VM, VM],
        out_specs=VM,
    )(inverse, columns.reshape(AY, AY))


def solution(mesh):
    placed = (
        P("shot", None, "depth", None, None),
        P("shot", None, "depth", None, None),
        P("shot", "depth", None, None),
        P("shot", "depth", None, None),
        P("shot", "depth", None, None),
        P("shot", "depth", None, None),
        P(),
        P(),
        P(),
        P(),
    )
    return jax.shard_map(
        shards, mesh=mesh, in_specs=placed, out_specs=P("shot", "depth", None), check_vma=False
    )
```

time: 358 us -> 91.1 us (0.25)
  waiting for transfers between devices: 223 us -> 13.1 us
  other arithmetic: 45.4 us -> 3.75 us
  starting transfers between devices: 66.5 us -> 34.8 us
  Pallas kernels: 0 us -> 30.2 us
  between operations: 14 us -> 0.19 us
    reduce_scatter x1 -> x0, waiting for transfers between devices: 215 us -> none  [shards(): lax.psum_scatter(jnp.einsum('kp,zky->pyz', selector, picture, precision=l...]
    ppermute x16 -> x6, starting transfers between devices: 53.7 us -> 15.7 us  [the longest x1 5.93 us: shards(): lax.ppermute(prev[:, :W - 1], 'depth', downward)]
    pallas_call x0 -> x4, Pallas kernels: none -> 30.2 us  [the longest x1 21.5 us: stencil(): pl.pallas_call(stencil_kernel, out_shape=jax.ShapeDtypeStruct((n, SLAB, A...]
    another operation x5 -> x6, other arithmetic: 22.8 us -> 1.22 us  [the longest x1 0.83 us: shards(): media_head = jnp.stack([part[:W - 1] for part in media])]
    add x10 -> x1, other arithmetic: 13.1 us -> 0.01 us  [shards(): held + jnp.sum(jnp.where(valid & (order == j), slot - held, 0), axis=1)]
    all_to_all x1 -> x2, waiting for transfers between devices: 0.01 us -> 12.7 us  [the longest x1 10.7 us: shards(): lax.all_to_all(send, 'shot', split_axis=0, concat_axis=0, tiled=True)]
    ppermute x16 -> x6, waiting for transfers between devices: 8.12 us -> 0.4 us  [the longest x1 0.38 us: shards(): lax.ppermute(prev[:, :W - 1], 'depth', downward)]
    all_to_all x1 -> x2, starting transfers between devices: 12.8 us -> 19 us  [the longest x1 11.4 us: shards(): lax.all_to_all(send, 'shot', split_axis=0, concat_axis=0, tiled=True)]
  transfers between devices with their start and end apart: 18 -> 8, of which waited for: 8 -> 3; matrix products, arithmetic and copies ran while one was open for 8% -> 9% of each run, Pallas kernels for 0% -> 6%
where the time goes in v1:
time: 91.1 us; the launch traced here: 90.7 us
  starting transfers between devices  34.8 us (38%)
  Pallas kernels  30.2 us (33%)
  waiting for transfers between devices  13.1 us (14%)
  local copies, waits for them, and re-layouts  8.65 us (9%)
  other arithmetic  3.75 us (4%)
    pallas_call x1, Pallas kernels, stencil(): pl.pallas_call(stencil_kernel, out_shape=jax.ShapeDtypeStruct((n, SLAB, A...  21.5 us
    all_to_all x1, starting transfers between devices, shards(): lax.all_to_all(send, 'shot', split_axis=0, concat_axis=0, tiled=True)  11.4 us
    all_to_all x1, waiting for transfers between devices, shards(): lax.all_to_all(send, 'shot', split_axis=0, concat_axis=0, tiled=True)  10.7 us
    all_to_all x1, starting transfers between devices, shards(): lax.all_to_all(pieces, 'depth', split_axis=0, concat_axis=0, tiled=True)  7.64 us
    ppermute x1, starting transfers between devices, shards(): lax.ppermute(prev[:, :W - 1], 'depth', downward)  5.93 us
    pallas_call x1, Pallas kernels, band_inverse(): pl.pallas_call(inverse_kernel, out_shape=jax.ShapeDtypeStruct((length, le...  5.12 us
    unnamed x32, local copies, waits for them, and re-layouts  4.26 us
    ppermute x1, starting transfers between devices, shards(): cur_high = lax.ppermute(cur, 'depth', downward)  4.17 us
  transfers between devices with their start and end apart: 8, of which 3 were waited for; matrix products, arithmetic and copies ran while one was open for 9% of the time, Pallas kernels for 6%

profile of v1, /device:TPU:1, one launch (start us, length us, event | category | flops | bytes accessed | tf_op | source)
XLA Modules:
  0.0 90.7 jit_solution(5071011002078368765)
XLA Ops:
  0.0 2.7 %collective-permute-start = (f32[2,8,64,128]{3,2,1,0:T(8,128)}, f32[2,8,64,128]{3,2,1,0:T(8,128)S(1)}, u32[]{:S(2)}, u32[]{:S(2)}) collective-permute-start(f32[2,8,64,128]{3,2,1,0:T(8,128)} %bitcast.23), channel_id=1, source_target_pairs={{0,1},{1,2},{2,3},{3,4},{4,5},{5,6},{6,7},{7,8},{8,9},{9,10},{10,1... | collective-permute-start | bytes 1572872 | tf_op jit(solution)/shard_map/ppermute | solution.py:279
  2.7 4.2 %collective-permute-start.3 = (f32[2,8,64,128]{3,2,1,0:T(8,128)}, f32[2,8,64,128]{3,2,1,0:T(8,128)S(1)}, u32[]{:S(2)}, u32[]{:S(2)}) collective-permute-start(f32[2,8,64,128]{3,2,1,0:T(8,128)} %bitcast.24), channel_id=1, source_target_pairs={{1,0},{2,1},{3,2},{4,3},{5,4},{6,5},{7,6},{8,7},{9,8},{10,9},{11,1... | collective-permute-start | bytes 1572872 | tf_op jit(solution)/shard_map/ppermute | solution.py:280
  6.8 1.1 %fusion.6 = (bf16[1,7,64,128]{3,2,1,0:T(8,128)(2,1)S(1)}, bf16[1,7,64,128]{3,2,1,0:T(8,128)(2,1)S(1)}, bf16[1,7,64,128]{3,2,1,0:T(8,128)(2,1)S(1)}, bf16[1,7,64,128]{3,2,1,0:T(8,128)(2,1)S(1)}) fusion(bf16[1,8,64,128]{3,2,1,0:T(8,128)(2,1)} %param.12, bf16[1,8,64,128]{3,2,1,0:T(8,128)(2,1)} %param.13), kind=kLoop, calls=%fused_computation.27 | loop fusion | bytes 917504 | tf_op jit(solution)/shard_map/slice | solution.py:278
  8.0 0.0 copy-done.3
  8.0 0.1 fusion.8
  8.1 0.1 pad_maximum_fusion
  8.2 0.0 copy-start
  8.2 0.0 collective-permute-start.2
  8.2 0.8 pad_maximum_fusion.1
  9.0 3.0 %collective-permute-start.5 = (bf16[4,7,64,128]{3,2,1,0:T(8,128)(2,1)}, bf16[4,7,64,128]{3,2,1,0:T(8,128)(2,1)S(1)}, u32[]{:S(2)}, u32[]{:S(2)}) collective-permute-start(bf16[4,7,64,128]{3,2,1,0:T(8,128)(2,1)} %pad_maximum_fusion.1), channel_id=1, source_target_pairs={{1,0},{2,1},{3,2},{4,3},{5,4},{6,5},{7,6},{8,7},{9,8},{10,9},{11,1... | collective-permute-start | bytes 1376264 | tf_op jit(solution)/shard_map/ppermute | solution.py:285
  12.0 0.9 fusion.5
  12.9 0.7 copy-done.13
  13.5 0.6 dynamic_slice.7
  14.1 0.7 copy-done.14
  14.8 0.6 broadcast_subtract_fusion
  15.4 0.1 dynamic_slice.6
  15.5 0.1 sub.63
  15.6 0.2 reduce_window_sum.18
  15.8 0.1 fusion.4
  15.8 0.0 copy-start.6
  15.9 5.9 %collective-permute-start.4 = (f32[2,7,64,128]{3,2,1,0:T(8,128)S(1)}, f32[2,7,64,128]{3,2,1,0:T(8,128)S(1)}, u32[]{:S(2)}, u32[]{:S(2)}) collective-permute-start(f32[2,7,64,128]{3,2,1,0:T(8,128)S(1)} %get-tuple-element.9), channel_id=1, source_target_pairs={{1,0},{2,1},{3,2},{4,3},{5,4},{6,5},{7,6},{8,7},{9,8},{10,9},{11,1... | collective-permute-start | bytes 1376264 | tf_op jit(solution)/shard_map/ppermute | solution.py:284
  21.8 0.1 select_reduce_fusion.1
  21.9 0.2 reduce_window_sum.17
  22.1 0.1 copy.14
  22.2 0.7 reshape.57.source
  22.9 0.6 add_convert_fusion.edge
  23.5 0.2 select_reduce_fusion.3
  23.7 0.4 collective-permute-done.4.prev_high
  24.1 0.3 copy-done.7
  24.4 0.2 copy-done.8
  24.6 0.3 copy-done.9
  24.8 0.2 copy-done.4
  25.0 0.1 copy-done.5
  25.2 21.5 %shard_map.101 = f32[64,8,128]{2,1,0:T(8,128)} custom-call(f32[2]{0:T(128)} %add_convert_fusion.edge, s32[64]{0:T(128)} %reshape.57.source, f32[2,8,64,128]{3,2,1,0:T(8,128)} %bitcast.25, f32[2,8,64,128]{3,2,1,0:T(8,128)} %bitcast.17, bf16[8,64,128]{2,1,0:T(8,128)(2,1)} %bitcast.19, bf16[8,64,128]{2,1,0:T(8,128)(2,1)} %bitcast.20, ...), custom_call_target="tpu_custom_call" | custom-call | tf_op jit(solution)/shard_map/pallas_call | solution.py:174
  46.6 11.4 %all-to-all-start = ((f32[64,8,128]{2,1,0:T(8,128)}), f32[64,8,128]{2,1,0:T(8,128)S(1)}, u32[]{:S(2)}, u32[]{:S(2)}) async-start(f32[64,8,128]{2,1,0:T(8,128)} %shard_map.101), calls=%async_computation | async-start | bytes 524288 | tf_op jit(solution)/shard_map/all_to_all | solution.py:306
  58.1 0.1 copy.13
  58.2 0.7 reshape.56.place
  58.9 0.2 convert_reduce_fusion
  59.0 0.5 copy-done.15
  59.5 10.7 %all-to-all-done.rows_in = f32[64,8,128]{2,1,0:T(8,128)S(1)} async-done(((f32[64,8,128]{2,1,0:T(8,128)}), f32[64,8,128]{2,1,0:T(8,128)S(1)}, u32[]{:S(2)}, u32[]{:S(2)}) %all-to-all-start) | async-done | bytes 262176 | tf_op jit(solution)/shard_map/all_to_all | solution.py:306
  70.3 0.7 copy-done.1
  71.0 1.9 %shard_map.102 = f32[16,8,128]{2,1,0:T(8,128)} custom-call(s32[64]{0:T(128)} %reshape.56.place, f32[64,8,128]{2,1,0:T(8,128)} %copy-done.1), custom_call_target="tpu_custom_call" | custom-call | tf_op jit(solution)/shard_map/pallas_call | solution.py:308
  72.9 7.6 %all-to-all-start.1 = ((f32[16,8,128]{2,1,0:T(8,128)}), f32[16,8,128]{2,1,0:T(8,128)S(1)}, u32[]{:S(2)}, u32[]{:S(2)}) async-start(f32[16,8,128]{2,1,0:T(8,128)} %shard_map.102), calls=%async_computation.1 | async-start | bytes 131072 | tf_op jit(solution)/shard_map/all_to_all | solution.py:315
  80.5 0.7 broadcast_select_fusion.jump
  81.2 5.1 %shard_map.100.inverse = f32[128,128]{1,0:T(8,128)} custom-call(f32[128,128]{1,0:T(8,128)} %broadcast_select_fusion.jump, f32[1,128]{1,0:T(1,128)} %bitcast.27), custom_call_target="tpu_custom_call" | custom-call | tf_op jit(solution)/shard_map/pallas_call | solution.py:221
  86.4 1.9 %all-to-all-done.1 = f32[16,8,128]{2,1,0:T(8,128)S(1)} async-done(((f32[16,8,128]{2,1,0:T(8,128)}), f32[16,8,128]{2,1,0:T(8,128)S(1)}, u32[]{:S(2)}, u32[]{:S(2)}) %all-to-all-start.1) | async-done | bytes 65568 | tf_op jit(solution)/shard_map/all_to_all | solution.py:315
  88.3 0.6 copy-done.10
  88.9 1.7 %shard_map.103 = f32[4,8,128]{2,1,0:T(8,128)} custom-call(f32[128,128]{1,0:T(8,128)} %shard_map.100.inverse, f32[128,128]{1,0:T(8,128)} %bitcast.26), custom_call_target="tpu_custom_call" | custom-call | tf_op jit(solution)/shard_map/pallas_call | solution.py:316
  (31 shorter events, 0.1 us)
Async XLA Ops:
  0.0 24.1 %collective-permute-start = (f32[2,8,64,128]{3,2,1,0:T(8,128)}, f32[2,8,64,128]{3,2,1,0:T(8,128)S(1)}, u32[]{:S(2)}, u32[]{:S(2)}) collective-permute-start(f32[2,8,64,128]{3,2,1,0:T(8,128)} %bitcast.23), channel_id=1, source_target_pairs={{0,1},{1,2},{2,3},{3,4},{4,5},{5,6},{6,7},{7,8},{8,9},{9,10},{10,1... | collective-permute-start | bytes 1572872 | tf_op jit(solution)/shard_map/ppermute | solution.py:279
  2.7 21.4 %collective-permute-start.3 = (f32[2,8,64,128]{3,2,1,0:T(8,128)}, f32[2,8,64,128]{3,2,1,0:T(8,128)S(1)}, u32[]{:S(2)}, u32[]{:S(2)}) collective-permute-start(f32[2,8,64,128]{3,2,1,0:T(8,128)} %bitcast.24), channel_id=1, source_target_pairs={{1,0},{2,1},{3,2},{4,3},{5,4},{6,5},{7,6},{8,7},{9,8},{10,9},{11,1... | collective-permute-start | bytes 1572872 | tf_op jit(solution)/shard_map/ppermute | solution.py:280
  6.8 1.1 %copy-start.2 = (bf16[1,8,64,128]{3,2,1,0:T(8,128)(2,1)S(1)}, bf16[1,8,64,128]{3,2,1,0:T(8,128)(2,1)}, u32[]{:S(2)}) copy-start(bf16[1,8,64,128]{3,2,1,0:T(8,128)(2,1)} %param.14) | copy-start | bytes 393220
  6.8 1.2 %copy-start.3 = (bf16[1,8,64,128]{3,2,1,0:T(8,128)(2,1)S(1)}, bf16[1,8,64,128]{3,2,1,0:T(8,128)(2,1)}, u32[]{:S(2)}) copy-start(bf16[1,8,64,128]{3,2,1,0:T(8,128)(2,1)} %param.15) | copy-start | bytes 393220
  8.2 3.8 %copy-start = (f32[1,2,8,64,128]{4,3,2,1,0:T(8,128)S(1)}, f32[1,2,8,64,128]{4,3,2,1,0:T(8,128)}, u32[]{:S(2)}) copy-start(f32[1,2,8,64,128]{4,3,2,1,0:T(8,128)} %param.10) | copy-start | bytes 1572868
  8.2 7.7 %collective-permute-start.2 = (bf16[4,7,64,128]{3,2,1,0:T(8,128)(2,1)S(1)}, bf16[4,7,64,128]{3,2,1,0:T(8,128)(2,1)S(1)}, u32[]{:S(2)}, u32[]{:S(2)}) collective-permute-start(bf16[4,7,64,128]{3,2,1,0:T(8,128)(2,1)S(1)} %pad_maximum_fusion), channel_id=1, source_target_pairs={{0,1},{1,2},{2,3},{3,4},{4,5},{5,6},{6,7},{7,8},{8,9},{9,10},{10,1... | collective-permute-start | bytes 1376264 | tf_op jit(solution)/shard_map/ppermute | solution.py:281
  9.0 14.6 %collective-permute-start.5 = (bf16[4,7,64,128]{3,2,1,0:T(8,128)(2,1)}, bf16[4,7,64,128]{3,2,1,0:T(8,128)(2,1)S(1)}, u32[]{:S(2)}, u32[]{:S(2)}) collective-permute-start(bf16[4,7,64,128]{3,2,1,0:T(8,128)(2,1)} %pad_maximum_fusion.1), channel_id=1, source_target_pairs={{1,0},{2,1},{3,2},{4,3},{5,4},{6,5},{7,6},{8,7},{9,8},{10,9},{11,1... | collective-permute-start | bytes 1376264 | tf_op jit(solution)/shard_map/ppermute | solution.py:285
  12.9 10.8 %collective-permute-start.1 = (f32[2,7,64,128]{3,2,1,0:T(8,128)}, f32[2,7,64,128]{3,2,1,0:T(8,128)S(1)}, u32[]{:S(2)}, u32[]{:S(2)}) collective-permute-start(f32[2,7,64,128]{3,2,1,0:T(8,128)} %get-tuple-element.10), channel_id=1, source_target_pairs={{0,1},{1,2},{2,3},{3,4},{4,5},{5,6},{6,7},{7,8},{8,9},{9,10},{10,1... | collective-permute-start | bytes 1376264 | tf_op jit(solution)/shard_map/ppermute | solution.py:281
  12.9 0.7 copy-start.13
  14.1 0.7 copy-start.14
  15.8 8.3 %copy-start.6 = (bf16[4,7,64,128]{3,2,1,0:T(8,128)(2,1)}, bf16[4,7,64,128]{3,2,1,0:T(8,128)(2,1)S(1)}, u32[]{:S(2)}) copy-start(bf16[4,7,64,128]{3,2,1,0:T(8,128)(2,1)S(1)} %collective-permute-done.2.media_low) | copy-start | bytes 1376260
  15.9 8.2 %collective-permute-start.4 = (f32[2,7,64,128]{3,2,1,0:T(8,128)S(1)}, f32[2,7,64,128]{3,2,1,0:T(8,128)S(1)}, u32[]{:S(2)}, u32[]{:S(2)}) collective-permute-start(f32[2,7,64,128]{3,2,1,0:T(8,128)S(1)} %get-tuple-element.9), channel_id=1, source_target_pairs={{1,0},{2,1},{3,2},{4,3},{5,4},{6,5},{7,6},{8,7},{9,8},{10,9},{11,1... | collective-permute-start | bytes 1376264 | tf_op jit(solution)/shard_map/ppermute | solution.py:284
  23.7 0.8 copy-start.7
  23.7 0.9 copy-start.8
  24.1 0.8 copy-start.9
  24.1 1.0 %copy-start.4 = (f32[2,8,64,128]{3,2,1,0:T(8,128)}, f32[2,8,64,128]{3,2,1,0:T(8,128)S(1)}, u32[]{:S(2)}) copy-start(f32[2,8,64,128]{3,2,1,0:T(8,128)S(1)} %collective-permute-done.cur_low) | copy-start | bytes 1572868
  24.1 1.1 %copy-start.5 = (f32[2,8,64,128]{3,2,1,0:T(8,128)}, f32[2,8,64,128]{3,2,1,0:T(8,128)S(1)}, u32[]{:S(2)}) copy-start(f32[2,8,64,128]{3,2,1,0:T(8,128)S(1)} %collective-permute-done.3.cur_high) | copy-start | bytes 1572868
  46.6 23.6 %all-to-all-start = ((f32[64,8,128]{2,1,0:T(8,128)}), f32[64,8,128]{2,1,0:T(8,128)S(1)}, u32[]{:S(2)}, u32[]{:S(2)}) async-start(f32[64,8,128]{2,1,0:T(8,128)} %shard_map.101), calls=%async_computation | async-start | bytes 524288 | tf_op jit(solution)/shard_map/all_to_all | solution.py:306
  58.2 0.7 copy-start.11
  58.9 0.7 copy-start.15
  59.5 21.0 %copy-start.12 = (f32[128]{0:T(128)}, f32[128]{0:T(128)S(1)}, u32[]{:S(2)}) copy-start(f32[128]{0:T(128)S(1)} %add_divide_fusion) | copy-start | bytes 1540
  70.3 0.7 copy-start.1
  72.9 15.4 %all-to-all-start.1 = ((f32[16,8,128]{2,1,0:T(8,128)}), f32[16,8,128]{2,1,0:T(8,128)S(1)}, u32[]{:S(2)}, u32[]{:S(2)}) async-start(f32[16,8,128]{2,1,0:T(8,128)} %shard_map.102), calls=%async_computation.1 | async-start | bytes 131072 | tf_op jit(solution)/shard_map/all_to_all | solution.py:315
  88.3 0.6 copy-start.10

commit v2 on v1

v2 whole, which is shorter than its diff:
```python
import jax
import jax.numpy as jnp
from jax import lax
from jax.experimental import pallas as pl
from jax.experimental.pallas import tpu as pltpu
from jax.sharding import PartitionSpec as P

NT = 8
W = 8
SLAB = 8
EXT = SLAB + 2 * W
AX = 64
AY = 128
PAD = 8
NEAR = 4
ROWS = 16
BODY = slice(PAD, PAD + AX)


def trig(angle):
    square = angle * angle
    sine = -1.0 / 39916800.0
    for term in (1.0 / 362880.0, -1.0 / 5040.0, 1.0 / 120.0, -1.0 / 6.0, 1.0):
        sine = sine * square + term
    cosine = 1.0 / 479001600.0
    for term in (-1.0 / 3628800.0, 1.0 / 40320.0, -1.0 / 720.0, 1.0 / 24.0, -0.5, 1.0):
        cosine = cosine * square + term
    return sine * angle, cosine


def weight_planes(speed, ratio, theta, sweep):
    sine, axis_z = trig(theta)
    half_sine, half_cosine = trig(0.5 * sweep)
    axis_x = sine * (1.0 - 2.0 * half_sine * half_sine)
    axis_y = sine * (2.0 * half_sine * half_cosine)
    tilted = -2.0 * ratio
    base = speed * (1.0 + 2.0 * ratio)
    tilted = speed * tilted
    cross = 0.5 * tilted
    zz = base + tilted * axis_z * axis_z
    xx = base + tilted * axis_x * axis_x
    yy = base + tilted * axis_y * axis_y
    zx = cross * axis_z * axis_x
    zy = cross * axis_z * axis_y
    xy = cross * axis_x * axis_y
    centre = 2.0 - 2.0 * (zz + xx + yy)
    lane = lax.broadcasted_iota(jnp.int32, speed.shape, 1)
    low = lane == 0
    high = lane == AY - 1

    def up(plane):
        return jnp.where(high, 0.0, pltpu.roll(plane, AY - 1, 1))

    def down(plane):
        return jnp.where(low, 0.0, pltpu.roll(plane, 1, 1))

    return (centre, zz, xx, zx, up(yy), up(-zy), up(-xy), down(yy), down(zy), down(xy))


def store_planes(planes, layer, parts, scale):
    for start in range(0, AX, 16):
        part = slice(start, start + 16)
        speed, ratio, theta, sweep = [ref[part].astype(jnp.float32) for ref in parts]
        for index, value in enumerate(weight_planes(speed * scale, ratio, theta, sweep)):
            planes[index, layer - 1, part, :] = value


def loop(first, last, body):
    def step(index, carry):
        body(index)
        return carry

    lax.fori_loop(first, last, step, 0)


def advance(source, target, planes, layer, start):
    part = slice(start, start + ROWS)
    (centre_w, zz, xx, zx, y_low, zy_low, xy_low, y_high, zy_high, xy_high) = [
        planes[i, layer - 1, part, :] for i in range(10)
    ]
    here = slice(PAD + start, PAD + start + ROWS)
    before = slice(PAD + start - 1, PAD + start + ROWS - 1)
    after = slice(PAD + start + 1, PAD + start + ROWS + 1)
    made = []
    for field in range(2):
        centre = source[field, layer, here, :]
        above = source[field, layer + 1, here, :]
        below = source[field, layer - 1, here, :]
        ahead = source[field, layer, after, :]
        behind = source[field, layer, before, :]
        step_z = above - below
        step_x = ahead - behind
        twist = (source[field, layer + 1, after, :] - source[field, layer + 1, before, :]) - (
            source[field, layer - 1, after, :] - source[field, layer - 1, before, :]
        )
        total = centre_w * centre - target[field, layer, here, :]
        total = total + zz * (above + below)
        total = total + xx * (ahead + behind)
        total = total + zx * twist
        total = total + pltpu.roll(y_low * centre + zy_low * step_z + xy_low * step_x, 1, 1)
        total = total + pltpu.roll(y_high * centre + zy_high * step_z + xy_high * step_x, AY - 1, 1)
        target[field, layer, here, :] = total
        made.append(total)
    return made


def advance_halo(source, target, planes, first, last):
    def halo(layer):
        for start in range(0, AX, ROWS):
            advance(source, target, planes, layer, start)

    if last > first:
        loop(first, last, halo)


def advance_own(source, target, planes, picture, fresh):
    def own(layer):
        for start in range(0, AX, ROWS):
            made = advance(source, target, planes, layer + W, start)
            place = pl.ds(pl.multiple_of(layer * AX + start, ROWS), ROWS)
            product = made[0] * made[1]
            picture[place, :] = product if fresh else picture[place, :] + product

    loop(0, SLAB, own)


def own_kernel(cur, prev, speed, ratio, tilt, azimuth, jump, column_scale, first, second, planes, inverse, stack):
    zeros = jnp.zeros((PAD, AY), jnp.float32)

    def clear(layer):
        for field in range(2):
            for buffer in (first, second):
                buffer[field, layer, 0:PAD, :] = zeros
                buffer[field, layer, PAD + AX : PAD + AX + PAD, :] = zeros

    def fill(layer):
        for field in range(2):
            first[field, layer + W, BODY, :] = cur[field, layer]
            second[field, layer + W, BODY, :] = prev[field, layer]
        store_planes(planes, layer + W, [ref.at[layer] for ref in (speed, ratio, tilt, azimuth)], 1.0)

    loop(0, EXT, clear)
    loop(0, SLAB, fill)
    invert(jump, column_scale, inverse, stack)


def take_halo(edge, fields_low, media_low, fields_high, media_high, first, second, planes, count, base_low, base_high):
    scales = (edge[0], edge[1])
    others = media_low.shape[1]
    for fields, media, scale, base, later in (
        (fields_low, media_low, scales[0], base_low, base_low + 1),
        (fields_high, media_high, scales[1], base_high, base_high - (base_high > W + SLAB)),
    ):
        def take(layer):
            for field in range(2):
                first[field, layer + base, BODY, :] = fields[field, layer] * scale

        def take_other(layer):
            for field in range(2):
                second[field, layer + later, BODY, :] = fields[field, layer + count] * scale
            store_planes(planes, layer + later, [media.at[i, layer] for i in range(4)], scale)

        loop(0, count, take)
        loop(0, others, take_other)


def near_kernel(
    edge, fields_low, media_low, fields_high, media_high, first_in, second_in, planes_in,
    first, second, planes, picture,
):
    take_halo(
        edge, fields_low, media_low, fields_high, media_high, first, second, planes, NEAR, W - NEAR, W + SLAB
    )
    for step in range(1, NEAR + 1):
        source, target = (first, second) if step % 2 else (second, first)
        advance_halo(source, target, planes, W - NEAR + step, W)
        advance_own(source, target, planes, picture, step == 1)
        advance_halo(source, target, planes, W + SLAB, W + SLAB + NEAR - step)


def far_kernel(
    edge, chosen, fields_low, media_low, fields_high, media_high, first_in, second_in, planes_in, picture_in,
    first, second, planes, picture, send,
):
    far = W - NEAR
    take_halo(
        edge, fields_low, media_low, fields_high, media_high, first, second, planes, far, 0, W + SLAB + NEAR
    )
    for step in range(1, NT + 1):
        source, target = (first, second) if step % 2 else (second, first)
        if step <= NEAR:
            advance_halo(source, target, planes, step, step + far)
            advance_halo(source, target, planes, EXT - step - far, EXT - step)
            continue
        advance_halo(source, target, planes, step, W)
        advance_own(source, target, planes, picture, False)
        advance_halo(source, target, planes, W + SLAB, EXT - step)
    for entry in range(chosen.shape[0]):
        send[entry] = picture[pl.ds(chosen[entry], SLAB, stride=AX), :]


VM = pl.BlockSpec(memory_space=pltpu.VMEM)
SM = pl.BlockSpec(memory_space=pltpu.SMEM)
DOUBLINGS = 14
GRANT = 28 << 20


def invert(jump, column_scale, inverse, stack):
    size = jump.shape[0]
    row = lax.broadcasted_iota(jnp.int32, (size, size), 0)
    column = lax.broadcasted_iota(jnp.int32, (size, size), 1)
    stack[0:size, :] = (row == column).astype(jnp.float32)
    stack[size : 2 * size, :] = jump[...]

    def double(counter, carry):
        grown = lax.dot_general(
            stack[...], stack[size : 2 * size, :], (((1,), (0,)), ((), ())),
            precision=lax.Precision.HIGHEST, preferred_element_type=jnp.float32,
        )
        stack[0:size, :] = stack[0:size, :] + grown[:size]
        stack[size : 2 * size, :] = grown[size:]
        return carry

    lax.fori_loop(0, DOUBLINGS, double, 0)
    inverse[...] = stack[0:size, :] * column_scale[...]


def band_parts(band_width, depth_damp):
    length = band_width.shape[0]
    index = jnp.arange(length, dtype=jnp.int32)
    distance = jnp.abs(index[:, None] - index[None, :])
    reach = jnp.maximum(band_width[:, None], band_width[None, :])
    adjacent = ((distance > 0) & (distance <= reach)).astype(jnp.float32)
    scale = 1.0 / (depth_damp + jnp.sum(adjacent, axis=1))
    return adjacent * scale[:, None], scale[None, :]


def gather_kernel(place, rows_in, out, held):
    for slot in range(held.shape[0]):
        held[slot] = jnp.zeros((SLAB, AY), jnp.float32)
    for entry in range(rows_in.shape[0]):
        slot = place[entry]
        held[slot] = held[slot] + rows_in[entry]
    slots = held.shape[0] - 1
    part = AY // out.shape[0]
    lane = lax.broadcasted_iota(jnp.int32, (SLAB, AY), 1)
    for piece in range(out.shape[0]):
        mixed = None
        for slot in range(slots):
            moved = held[slot]
            turn = (slot * part - piece * part) % AY
            if turn:
                moved = pltpu.roll(moved, turn, 1)
            mixed = moved if mixed is None else jnp.where(lane >= slot * part, moved, mixed)
        out[piece] = mixed * (1.0 / NT)


def apply_kernel(inverse, columns, out):
    solved = lax.dot_general(
        columns[...], inverse[...], (((0,), (1,)), ((), ())),
        precision=lax.Precision.HIGHEST, preferred_element_type=jnp.float32,
    )
    slots, part = out.shape[:2]
    for slot in range(slots):
        out[slot] = solved[slot * part : (slot + 1) * part]


def pick_rows(blocks, anchors):
    row = blocks - anchors
    valid = (row >= 0) & (row < AX)
    order = jnp.cumsum(valid.astype(jnp.int32), axis=1) - 1
    return row, valid, order


def shards(
    prev_fields, cur_fields, speed_term, epsilon, tilt, azimuth,
    aperture_anchor, slot_block, band_width, depth_damp,
):
    depth = lax.axis_size("depth")
    shots = lax.axis_size("shot")
    upward = [(i, (i + 1) % depth) for i in range(depth)]
    downward = [((i + 1) % depth, i) for i in range(depth)]
    prev, cur = prev_fields[0], cur_fields[0]
    media = [speed_term[0], epsilon[0], tilt[0], azimuth[0]]

    def cut(parts, first, last):
        return jnp.stack([part[first:last] for part in parts])

    def fields(cur_first, cur_last, prev_first, prev_last):
        return jnp.concatenate([cur[:, cur_first:cur_last], prev[:, prev_first:prev_last]], axis=1)

    def exchange(up, down):
        return lax.ppermute(up, "depth", upward), lax.ppermute(down, "depth", downward)

    far = SLAB - NEAR
    near_fields = exchange(fields(far, SLAB, far + 1, SLAB), fields(0, NEAR, 0, NEAR - 1))
    near_media = exchange(cut(media, far + 1, SLAB), cut(media, 0, NEAR - 1))
    far_fields = exchange(fields(0, far, 1, far + 1), fields(NEAR, SLAB, NEAR - 1, SLAB - 1))
    far_media = exchange(cut(media, 1, far + 1), cut(media, NEAR - 1, SLAB - 1))
    my_depth = lax.axis_index("depth")
    my_shot = lax.axis_index("shot")
    edge = jnp.stack([my_depth > 0, my_depth < depth - 1]).astype(jnp.float32)

    held = slot_block.shape[0] // shots
    blocks = slot_block.reshape(shots, held)
    row, valid, order = pick_rows(blocks, aperture_anchor[my_shot])
    source = jnp.stack(
        [jnp.sum(jnp.where(valid & (order == j), row, 0), axis=1) for j in range(2)], axis=1
    ).reshape(-1)
    mine = lax.dynamic_slice_in_dim(slot_block, my_shot * held, held)
    row, valid, order = pick_rows(mine[None, :], aperture_anchor[:, None])
    slot = jnp.arange(held, dtype=jnp.int32)[None, :]
    place = jnp.stack(
        [held + jnp.sum(jnp.where(valid & (order == j), slot - held, 0), axis=1) for j in range(2)], axis=1
    ).reshape(-1)

    length = band_width.shape[0]
    buffer = jax.ShapeDtypeStruct((2, EXT, AX + 2 * PAD, AY), jnp.float32)
    plane = jax.ShapeDtypeStruct((10, EXT - 2, AX, AY), jnp.float32)
    square = jax.ShapeDtypeStruct((length, length), jnp.float32)
    image = jax.ShapeDtypeStruct((SLAB * AX, AY), jnp.float32)
    sent = jax.ShapeDtypeStruct((2 * shots, SLAB, AY), jnp.float32)
    grant = pltpu.CompilerParams(vmem_limit_bytes=GRANT)
    first, second, planes, inverse = pl.pallas_call(
        own_kernel,
        out_shape=(buffer, buffer, plane, square),
        in_specs=[VM] * 8,
        out_specs=[VM] * 4,
        scratch_shapes=[pltpu.VMEM((2 * length, length), jnp.float32)],
        compiler_params=grant,
    )(cur, prev, *media, *band_parts(band_width, depth_damp))
    first, second, planes, picture = pl.pallas_call(
        near_kernel,
        out_shape=(buffer, buffer, plane, image),
        in_specs=[SM] + [VM] * 7,
        out_specs=[VM] * 4,
        input_output_aliases={5: 0, 6: 1, 7: 2},
        compiler_params=grant,
    )(edge, near_fields[0], near_media[0], near_fields[1], near_media[1], first, second, planes)
    send = pl.pallas_call(
        far_kernel,
        out_shape=(buffer, buffer, plane, image, sent),
        in_specs=[SM, SM] + [VM] * 8,
        out_specs=[VM] * 5,
        input_output_aliases={6: 0, 7: 1, 8: 2, 9: 3},
        compiler_params=grant,
    )(edge, source, far_fields[0], far_media[0], far_fields[1], far_media[1], first, second, planes, picture)[4]
    received = lax.all_to_all(send, "shot", split_axis=0, concat_axis=0, tiled=True)
    part = AY // depth
    pieces = pl.pallas_call(
        gather_kernel,
        out_shape=jax.ShapeDtypeStruct((depth, SLAB, AY), jnp.float32),
        in_specs=[SM, VM],
        out_specs=VM,
        scratch_shapes=[pltpu.VMEM((held + 1, SLAB, AY), jnp.float32)],
        compiler_params=grant,
    )(place, received)
    columns = lax.all_to_all(pieces, "depth", split_axis=0, concat_axis=0, tiled=True)
    return pl.pallas_call(
        apply_kernel,
        out_shape=jax.ShapeDtypeStruct((held, part, AY), jnp.float32),
        in_specs=[VM, VM],
        out_specs=VM,
        compiler_params=grant,
    )(inverse, columns.reshape(AY, AY))


def solution(mesh):
    placed = (
        P("shot", None, "depth", None, None),
        P("shot", None, "depth", None, None),
        P("shot", "depth", None, None),
        P("shot", "depth", None, None),
        P("shot", "depth", None, None),
        P("shot", "depth", None, None),
        P(),
        P(),
        P(),
        P(),
    )
    return jax.shard_map(
        shards, mesh=mesh, in_specs=placed, out_specs=P("shot", "depth", None), check_vma=False
    )
```

time: 91.1 us -> 107 us (1.17)
  blocking collectives: 0 us -> 19.3 us
  other arithmetic: 3.75 us -> 17.8 us
  starting transfers between devices: 34.8 us -> 23.3 us
  Pallas kernels: 30.2 us -> 26.4 us
  waiting for transfers between devices: 13.1 us -> 10 us
    all_to_all x0 -> x1, blocking collectives: none -> 19.3 us  [shards(): lax.all_to_all(pieces, 'depth', split_axis=0, concat_axis=0, tiled=True)]
    all_to_all x1 -> x0, starting transfers between devices: 7.64 us -> none  [shards(): lax.all_to_all(pieces, 'depth', split_axis=0, concat_axis=0, tiled=True)]
    concatenate x0 -> x4, other arithmetic: none -> 4.3 us  [fields(): jnp.concatenate([cur[:, cur_first:cur_last], prev[:, prev_first:prev_last...]
    all_to_all x1, starting transfers between devices: 11.4 us -> 7.54 us  [shards(): lax.all_to_all(send, 'shot', split_axis=0, concat_axis=0, tiled=True)]
    unnamed x32 -> x34, local copies, waits for them, and re-layouts: 4.26 us -> 0.75 us
    another operation x2 -> x4, other arithmetic: 0.89 us -> 4.07 us  [cut(): return jnp.stack([part[first:last] for part in parts])]
    slice x3 -> x6, local copies, waits for them, and re-layouts: 2.07 us -> 5.18 us  [the longest x4 3.3 us: cut(): return jnp.stack([part[first:last] for part in parts])]
    another operation x2, other arithmetic: 0.31 us -> 2.96 us  [pick_rows(): order = jnp.cumsum(valid.astype(jnp.int32), axis=1) - 1]
  transfers between devices with their start and end apart: 8 -> 9, of which waited for: 3 -> 1; matrix products, arithmetic and copies ran while one was open for 9% -> 23% of each run, Pallas kernels for 6% -> 12%
where the time goes in v2:
time: 107 us
  Pallas kernels  26.4 us (25%)
  starting transfers between devices  23.3 us (22%)
  blocking collectives  19.3 us (18%)
  other arithmetic  17.8 us (17%)
  waiting for transfers between devices  10 us (9%)
  local copies, waits for them, and re-layouts  9.64 us (9%)
    all_to_all x1, blocking collectives, shards(): lax.all_to_all(pieces, 'depth', split_axis=0, concat_axis=0, tiled=True)  19.3 us
    ppermute x4, starting transfers between devices, exchange(): lax.ppermute(down, 'depth', downward)  13 us
    pallas_call x1, Pallas kernels, shards(): pl.pallas_call(far_kernel, out_shape=(buffer, buffer, plane, image, sent)...  12.1 us
    all_to_all x1, waiting for transfers between devices, shards(): lax.all_to_all(send, 'shot', split_axis=0, concat_axis=0, tiled=True)  9.99 us
    all_to_all x1, starting transfers between devices, shards(): lax.all_to_all(send, 'shot', split_axis=0, concat_axis=0, tiled=True)  7.54 us
    pallas_call x1, Pallas kernels, shards(): pl.pallas_call(near_kernel, out_shape=(buffer, buffer, plane, image), in_...  7.27 us
    pallas_call x1, Pallas kernels, shards(): pl.pallas_call(own_kernel, out_shape=(buffer, buffer, plane, square), in_...  5.2 us
    concatenate x4, other arithmetic, fields(): jnp.concatenate([cur[:, cur_first:cur_last], prev[:, prev_first:prev_last...  4.3 us
  transfers between devices with their start and end apart: 9, of which 1 were waited for; matrix products, arithmetic and copies ran while one was open for 23% of the time, Pallas kernels for 12%

profile of v2, /device:TPU:1, one launch (start us, length us, event | category | flops | bytes accessed | tf_op | source)
XLA Modules:
  0.0 106.7 jit_solution(7195950317558060808)
XLA Ops:
  0.0 1.0 fusion.8
  1.0 0.9 fusion.10
  1.9 0.7 pad_maximum_fusion.6
  2.6 2.7 %collective-permute-start.5 = (bf16[4,3,64,128]{3,2,1,0:T(8,128)(2,1)}, bf16[4,3,64,128]{3,2,1,0:T(8,128)(2,1)S(1)}, u32[]{:S(2)}, u32[]{:S(2)}) collective-permute-start(bf16[4,3,64,128]{3,2,1,0:T(8,128)(2,1)} %pad_maximum_fusion.6), channel_id=1, source_target_pairs={{0,1},{1,2},{2,3},{3,4},{4,5},{5,6},{6,7},{7,8},{8,9},{9,10},{10,1... | collective-permute-start | bytes 589832 | tf_op jit(solution)/shard_map/ppermute | solution.py:293
  5.3 0.7 pad_maximum_fusion.7
  6.0 4.2 %collective-permute-start.7 = (bf16[4,3,64,128]{3,2,1,0:T(8,128)(2,1)}, bf16[4,3,64,128]{3,2,1,0:T(8,128)(2,1)}, u32[]{:S(2)}, u32[]{:S(2)}) collective-permute-start(bf16[4,3,64,128]{3,2,1,0:T(8,128)(2,1)} %pad_maximum_fusion.7), channel_id=1, source_target_pairs={{1,0},{2,1},{3,2},{4,3},{5,4},{6,5},{7,6},{8,7},{9,8},{10,9},{11,1... | collective-permute-start | bytes 589832 | tf_op jit(solution)/shard_map/ppermute | solution.py:293
  10.1 1.0 fusion.5
  11.2 0.8 fusion.6
  12.0 0.0 copy-start.11
  12.1 0.8 pad_maximum_fusion.2
  12.9 0.8 pad_maximum_fusion.3
  13.7 3.0 %collective-permute-start.6 = (f32[2,7,64,128]{3,2,1,0:T(8,128)}, f32[2,7,64,128]{3,2,1,0:T(8,128)S(1)}, u32[]{:S(2)}, u32[]{:S(2)}) collective-permute-start(f32[2,7,64,128]{3,2,1,0:T(8,128)} %pad_maximum_fusion.3), channel_id=1, source_target_pairs={{1,0},{2,1},{3,2},{4,3},{5,4},{6,5},{7,6},{8,7},{9,8},{10,9},{11,1... | collective-permute-start | bytes 1376264 | tf_op jit(solution)/shard_map/ppermute | solution.py:293
  16.7 0.8 pad_maximum_fusion
  17.6 0.7 fusion.12
  18.3 0.7 fusion.14
  19.0 0.8 convert_reduce_fusion
  19.8 0.6 dynamic_slice.7
  20.4 1.2 %broadcast_subtract_fusion = s32[128]{0:T(128)} fusion(s32[128]{0:T(128)S(1)} %copy-done.16, s32[]{:T(128)} %bitcast.11), kind=kLoop, calls=%fused_computation.31 | loop fusion | flops 128 | bytes 1028 | tf_op jit(solution)/shard_map/sub | solution.py:269
  21.5 0.7 sub.63
  22.2 0.6 fusion.3
  22.8 1.5 %reduce_window_sum.18 = s32[32,4]{1,0:T(8,128)} reduce-window(s32[32,4]{1,0:T(8,128)} %fusion.3, s32[]{:T(128)} %constant.14.clone.1), window={size=1x4 pad=0_0x3_0}, to_apply=%region_4.5 | reduce-window | flops 384 | bytes 1028 | tf_op jit(solution)/shard_map/jit(cumsum)/reduce_window_sum | solution.py:271
  24.3 1.8 %pad_maximum_fusion.1 = f32[2,8,64,128]{3,2,1,0:T(8,128)} fusion(f32[2,4,64,128]{3,2,1,0:T(8,128)} %get-tuple-element.52, f32[2,4,64,128]{3,2,1,0:T(8,128)S(1)} %get-tuple-element.29), kind=kLoop, calls=%fused_computation.1 | loop fusion | flops 131072 | bytes 1048576 | tf_op jit(solution)/shard_map/concatenate | solution.py:290
  26.1 0.7 dynamic_slice.6
  26.9 1.3 %fusion.4 = s32[32,4]{1,0:T(8,128)} fusion(s32[32]{0:T(128)} %param.16, s32[4]{0:T(128)S(1)} %dynamic_slice.6), kind=kLoop, calls=%fused_computation.23 | loop fusion | flops 640 | bytes 656 | tf_op jit(solution)/shard_map/convert_element_type | solution.py:271
  28.2 1.6 %pad_maximum_fusion.4 = bf16[4,4,64,128]{3,2,1,0:T(8,128)(2,1)} fusion(bf16[1,4,64,128]{3,2,1,0:T(8,128)(2,1)} %get-tuple-element.55, bf16[1,4,64,128]{3,2,1,0:T(8,128)(2,1)} %get-tuple-element.46, bf16[1,4,64,128]{3,2,1,0:T(8,128)(2,1)} %get-tuple-element.53, bf16[1,4,64,128]{3,2,1,0:T(8,128)(2,1)S(1)} %get-tuple-element.42), kind=kLoop, calls=%fused_computation.4 | loop fusion | flops 393216 | bytes 524288 | tf_op jit(solution)/shard_map/stack | solution.py:287
  29.8 0.8 select_reduce_fusion.1
  30.7 0.7 add_divide_fusion
  31.4 0.7 copy-done.6
  32.0 3.0 %collective-permute-start.2 = (f32[2,8,64,128]{3,2,1,0:T(8,128)}, f32[2,8,64,128]{3,2,1,0:T(8,128)S(1)}, u32[]{:S(2)}, u32[]{:S(2)}) collective-permute-start(f32[2,8,64,128]{3,2,1,0:T(8,128)} %pad_maximum_fusion.1), channel_id=1, source_target_pairs={{1,0},{2,1},{3,2},{4,3},{5,4},{6,5},{7,6},{8,7},{9,8},{10,9},{11,1... | collective-permute-start | bytes 1572872 | tf_op jit(solution)/shard_map/ppermute | solution.py:293
  35.0 0.7 copy.21
  35.7 0.8 reshape.73.chosen
  36.5 1.5 %reduce_window_sum.17 = s32[32,4]{1,0:T(8,128)} reduce-window(s32[32,4]{1,0:T(8,128)} %fusion.4, s32[]{:T(128)} %constant.14.clone.1), window={size=1x4 pad=0_0x3_0}, to_apply=%region_1.2 | reduce-window | flops 384 | bytes 1028 | tf_op jit(solution)/shard_map/jit(cumsum)/reduce_window_sum | solution.py:271
  38.0 1.0 pad_maximum_fusion.5
  39.0 0.0 collective-permute-start.1
  39.1 3.0 %collective-permute-start.3 = (bf16[4,4,64,128]{3,2,1,0:T(8,128)(2,1)S(1)}, bf16[4,4,64,128]{3,2,1,0:T(8,128)(2,1)S(1)}, u32[]{:S(2)}, u32[]{:S(2)}) collective-permute-start(bf16[4,4,64,128]{3,2,1,0:T(8,128)(2,1)S(1)} %pad_maximum_fusion.5), channel_id=1, source_target_pairs={{1,0},{2,1},{3,2},{4,3},{5,4},{6,5},{7,6},{8,7},{9,8},{10,9},{11,1... | collective-permute-start | bytes 786440 | tf_op jit(solution)/shard_map/ppermute | solution.py:293
  42.0 0.8 broadcast_select_fusion.jump
  42.9 5.2 %shard_map.100 = (f32[2,24,80,128]{3,2,1,0:T(8,128)S(1)}, f32[2,24,80,128]{3,2,1,0:T(8,128)S(1)}, f32[10,22,64,128]{3,2,1,0:T(8,128)S(1)}, f32[128,128]{1,0:T(8,128)S(1)}) custom-call(f32[2,8,64,128]{3,2,1,0:T(8,128)S(1)} %bitcast.21, f32[2,8,64,128]{3,2,1,0:T(8,128)S(1)} %bitcast.19, bf16[8,64,128]{2,1,0:T(8,128)(2,1)S(1)} %bitcast.22, ...), custom_call_target="tpu_custom_call" | custom-call | tf_op jit(solution)/shard_map/pallas_call | solution.py:324
  48.1 0.1 add_convert_fusion.edge
  48.2 7.3 %shard_map.101 = (f32[2,24,80,128]{3,2,1,0:T(8,128)S(1)}, f32[2,24,80,128]{3,2,1,0:T(8,128)S(1)}, f32[10,22,64,128]{3,2,1,0:T(8,128)S(1)}, f32[512,128]{1,0:T(8,128)S(1)}) custom-call(f32[2]{0:T(128)S(1)} %add_convert_fusion.edge, ...), custom_call_target="tpu_custom_call", output_to_operand_aliasing={{0}: (5, {}), {1}: (6, {}), {2}: (7, {})} | custom-call | tf_op jit(solution)/shard_map/pallas_call | solution.py:332
  55.5 12.1 %shard_map.102 = (f32[2,24,80,128]{3,2,1,0:T(8,128)S(1)}, f32[2,24,80,128]{3,2,1,0:T(8,128)S(1)}, f32[10,22,64,128]{3,2,1,0:T(8,128)S(1)}, f32[512,128]{1,0:T(8,128)S(1)}, f32[64,8,128]{2,1,0:T(8,128)}) custom-call(f32[2]{0:T(128)S(1)} %add_convert_fusion.edge, ...), custom_call_target="tpu_custom_call", output_to_operand_aliasing={{0}: (6, {}), {1}: (7, {}), {2}: (8, {}), {3}: (9, {})} | custom-call | tf_op jit(solution)/shard_map/pallas_call | solution.py:340
  67.6 7.5 %all-to-all-start = ((f32[64,8,128]{2,1,0:T(8,128)}), f32[64,8,128]{2,1,0:T(8,128)S(1)}, u32[]{:S(2)}, u32[]{:S(2)}) async-start(f32[64,8,128]{2,1,0:T(8,128)} %get-tuple-element.22), calls=%async_computation | async-start | bytes 524288 | tf_op jit(solution)/shard_map/all_to_all | solution.py:348
  75.2 0.2 select_reduce_fusion.3
  75.4 0.1 copy.20
  75.5 0.1 reshape.72.place
  75.6 10.0 %all-to-all-done.rows_in = f32[64,8,128]{2,1,0:T(8,128)S(1)} async-done(((f32[64,8,128]{2,1,0:T(8,128)}), f32[64,8,128]{2,1,0:T(8,128)S(1)}, u32[]{:S(2)}, u32[]{:S(2)}) %all-to-all-start) | async-done | bytes 262176 | tf_op jit(solution)/shard_map/all_to_all | solution.py:348
  85.6 0.9 shard_map.103
  86.6 19.3 %all_to_all.10 = f32[16,8,128]{2,1,0:T(8,128)S(1)} all-to-all(f32[16,8,128]{2,1,0:T(8,128)S(1)} %shard_map.103), channel_id=1, replica_groups=mesh['shot'=32,'depth'=16] {'depth'}, dimensions={0} | all-to-all | bytes 131072 | tf_op jit(solution)/shard_map/all_to_all | solution.py:358
  105.8 0.9 shard_map.104
  (46 shorter events, 0.1 us)
Async XLA Ops:
  0.0 11.2 %copy-start = (f32[1,2,8,64,128]{4,3,2,1,0:T(8,128)S(1)}, f32[1,2,8,64,128]{4,3,2,1,0:T(8,128)}, u32[]{:S(2)}) copy-start(f32[1,2,8,64,128]{4,3,2,1,0:T(8,128)} %param.10) | copy-start | bytes 1572868
  0.0 11.2 %copy-start.1 = (f32[1,2,8,64,128]{4,3,2,1,0:T(8,128)S(1)}, f32[1,2,8,64,128]{4,3,2,1,0:T(8,128)}, u32[]{:S(2)}) copy-start(f32[1,2,8,64,128]{4,3,2,1,0:T(8,128)} %param.11) | copy-start | bytes 1572868
  2.6 28.8 %collective-permute-start.5 = (bf16[4,3,64,128]{3,2,1,0:T(8,128)(2,1)}, bf16[4,3,64,128]{3,2,1,0:T(8,128)(2,1)S(1)}, u32[]{:S(2)}, u32[]{:S(2)}) collective-permute-start(bf16[4,3,64,128]{3,2,1,0:T(8,128)(2,1)} %pad_maximum_fusion.6), channel_id=1, source_target_pairs={{0,1},{1,2},{2,3},{3,4},{4,5},{5,6},{6,7},{7,8},{8,9},{9,10},{10,1... | collective-permute-start | bytes 589832 | tf_op jit(solution)/shard_map/ppermute | solution.py:293
  6.0 33.1 %collective-permute-start.7 = (bf16[4,3,64,128]{3,2,1,0:T(8,128)(2,1)}, bf16[4,3,64,128]{3,2,1,0:T(8,128)(2,1)}, u32[]{:S(2)}, u32[]{:S(2)}) collective-permute-start(bf16[4,3,64,128]{3,2,1,0:T(8,128)(2,1)} %pad_maximum_fusion.7), channel_id=1, source_target_pairs={{1,0},{2,1},{3,2},{4,3},{5,4},{6,5},{7,6},{8,7},{9,8},{10,9},{11,1... | collective-permute-start | bytes 589832 | tf_op jit(solution)/shard_map/ppermute | solution.py:293
  12.0 5.5 %copy-start.2 = (bf16[1,8,64,128]{3,2,1,0:T(8,128)(2,1)S(1)}, bf16[1,8,64,128]{3,2,1,0:T(8,128)(2,1)}, u32[]{:S(2)}) copy-start(bf16[1,8,64,128]{3,2,1,0:T(8,128)(2,1)} %param.12) | copy-start | bytes 393220
  12.0 5.5 %copy-start.3 = (bf16[1,8,64,128]{3,2,1,0:T(8,128)(2,1)S(1)}, bf16[1,8,64,128]{3,2,1,0:T(8,128)(2,1)}, u32[]{:S(2)}) copy-start(bf16[1,8,64,128]{3,2,1,0:T(8,128)(2,1)} %param.13) | copy-start | bytes 393220
  12.0 6.2 %copy-start.4 = (bf16[1,8,64,128]{3,2,1,0:T(8,128)(2,1)S(1)}, bf16[1,8,64,128]{3,2,1,0:T(8,128)(2,1)}, u32[]{:S(2)}) copy-start(bf16[1,8,64,128]{3,2,1,0:T(8,128)(2,1)} %param.14) | copy-start | bytes 393220
  12.0 6.2 %copy-start.5 = (bf16[1,8,64,128]{3,2,1,0:T(8,128)(2,1)S(1)}, bf16[1,8,64,128]{3,2,1,0:T(8,128)(2,1)}, u32[]{:S(2)}) copy-start(bf16[1,8,64,128]{3,2,1,0:T(8,128)(2,1)} %param.15) | copy-start | bytes 393220
  12.0 7.0 %copy-start.11 = (s32[128]{0:T(128)S(1)}, s32[128]{0:T(128)}, u32[]{:S(2)}) copy-start(s32[128]{0:T(128)} %param.18) | copy-start | bytes 1540
  12.1 7.7 %copy-start.12 = (s32[32]{0:T(128)S(1)}, s32[32]{0:T(128)}, u32[]{:S(2)}) copy-start(s32[32]{0:T(128)} %param.16) | copy-start | bytes 388
  12.1 8.3 %copy-start.16 = (s32[128]{0:T(128)S(1)}, s32[128]{0:T(128)}, u32[]{:S(2)}) copy-start(s32[128]{0:T(128)} %param.17) | copy-start | bytes 1540
  12.9 26.2 %collective-permute-start.4 = (f32[2,7,64,128]{3,2,1,0:T(8,128)}, f32[2,7,64,128]{3,2,1,0:T(8,128)S(1)}, u32[]{:S(2)}, u32[]{:S(2)}) collective-permute-start(f32[2,7,64,128]{3,2,1,0:T(8,128)} %pad_maximum_fusion.2), channel_id=1, source_target_pairs={{0,1},{1,2},{2,3},{3,4},{4,5},{5,6},{6,7},{7,8},{8,9},{9,10},{10,1... | collective-permute-start | bytes 1376264 | tf_op jit(solution)/shard_map/ppermute | solution.py:293
  13.7 34.4 %collective-permute-start.6 = (f32[2,7,64,128]{3,2,1,0:T(8,128)}, f32[2,7,64,128]{3,2,1,0:T(8,128)S(1)}, u32[]{:S(2)}, u32[]{:S(2)}) collective-permute-start(f32[2,7,64,128]{3,2,1,0:T(8,128)} %pad_maximum_fusion.3), channel_id=1, source_target_pairs={{1,0},{2,1},{3,2},{4,3},{5,4},{6,5},{7,6},{8,7},{9,8},{10,9},{11,1... | collective-permute-start | bytes 1376264 | tf_op jit(solution)/shard_map/ppermute | solution.py:293
  17.5 37.9 %collective-permute-start = (f32[2,8,64,128]{3,2,1,0:T(8,128)}, f32[2,8,64,128]{3,2,1,0:T(8,128)S(1)}, u32[]{:S(2)}, u32[]{:S(2)}) collective-permute-start(f32[2,8,64,128]{3,2,1,0:T(8,128)} %pad_maximum_fusion), channel_id=1, source_target_pairs={{0,1},{1,2},{2,3},{3,4},{4,5},{5,6},{6,7},{7,8},{8,9},{9,10},{10,1... | collective-permute-start | bytes 1572872 | tf_op jit(solution)/shard_map/ppermute | solution.py:293
  26.9 4.5 %copy-start.14 = (s32[4]{0:T(128)}, s32[4]{0:T(128)S(1)}, u32[]{:S(2)}) copy-start(s32[4]{0:T(128)S(1)} %dynamic_slice.6) | copy-start | bytes 52
  31.4 0.7 copy-start.6
  32.0 23.4 %collective-permute-start.2 = (f32[2,8,64,128]{3,2,1,0:T(8,128)}, f32[2,8,64,128]{3,2,1,0:T(8,128)S(1)}, u32[]{:S(2)}, u32[]{:S(2)}) collective-permute-start(f32[2,8,64,128]{3,2,1,0:T(8,128)} %pad_maximum_fusion.1), channel_id=1, source_target_pairs={{1,0},{2,1},{3,2},{4,3},{5,4},{6,5},{7,6},{8,7},{9,8},{10,9},{11,1... | collective-permute-start | bytes 1572872 | tf_op jit(solution)/shard_map/ppermute | solution.py:293
  38.0 10.2 %copy-start.7 = (bf16[4,3,64,128]{3,2,1,0:T(8,128)(2,1)S(1)}, bf16[4,3,64,128]{3,2,1,0:T(8,128)(2,1)}, u32[]{:S(2)}) copy-start(bf16[4,3,64,128]{3,2,1,0:T(8,128)(2,1)} %copy-done.6) | copy-start | bytes 589828
  39.0 16.4 %collective-permute-start.1 = (bf16[4,4,64,128]{3,2,1,0:T(8,128)(2,1)}, bf16[4,4,64,128]{3,2,1,0:T(8,128)(2,1)S(1)}, u32[]{:S(2)}, u32[]{:S(2)}) collective-permute-start(bf16[4,4,64,128]{3,2,1,0:T(8,128)(2,1)} %pad_maximum_fusion.4), channel_id=1, source_target_pairs={{0,1},{1,2},{2,3},{3,4},{4,5},{5,6},{6,7},{7,8},{8,9},{9,10},{10,1... | collective-permute-start | bytes 786440 | tf_op jit(solution)/shard_map/ppermute | solution.py:293
  39.1 16.4 %collective-permute-start.3 = (bf16[4,4,64,128]{3,2,1,0:T(8,128)(2,1)S(1)}, bf16[4,4,64,128]{3,2,1,0:T(8,128)(2,1)S(1)}, u32[]{:S(2)}, u32[]{:S(2)}) collective-permute-start(bf16[4,4,64,128]{3,2,1,0:T(8,128)(2,1)S(1)} %pad_maximum_fusion.5), channel_id=1, source_target_pairs={{1,0},{2,1},{3,2},{4,3},{5,4},{6,5},{7,6},{8,7},{9,8},{10,9},{11,1... | collective-permute-start | bytes 786440 | tf_op jit(solution)/shard_map/ppermute | solution.py:293
  48.1 7.4 %copy-start.8 = (f32[128,128]{1,0:T(8,128)}, f32[128,128]{1,0:T(8,128)S(1)}, u32[]{:S(2)}) copy-start(f32[128,128]{1,0:T(8,128)S(1)} %get-tuple-element.14.inverse) | copy-start | bytes 196612
  55.5 19.7 %copy-start.10 = (s32[32,4]{1,0:T(8,128)S(1)}, s32[32,4]{1,0:T(8,128)}, u32[]{:S(2)}) copy-start(s32[32,4]{1,0:T(8,128)} %reduce_window_sum.17) | copy-start | bytes 1540
  55.5 19.7 %copy-start.13 = (s32[32]{0:T(128)S(1)}, s32[32]{0:T(128)}, u32[]{:S(2)}) copy-start(s32[32]{0:T(128)} %param.16) | copy-start | bytes 388
  55.5 19.7 %copy-start.15 = (s32[4]{0:T(128)S(1)}, s32[4]{0:T(128)}, u32[]{:S(2)}) copy-start(s32[4]{0:T(128)} %copy-done.14) | copy-start | bytes 52
  55.5 50.3 %copy-start.9 = (f32[128,128]{1,0:T(8,128)S(1)}, f32[128,128]{1,0:T(8,128)}, u32[]{:S(2)}) copy-start(f32[128,128]{1,0:T(8,128)} %copy-done.8) | copy-start | bytes 196612
  67.6 18.0 %all-to-all-start = ((f32[64,8,128]{2,1,0:T(8,128)}), f32[64,8,128]{2,1,0:T(8,128)S(1)}, u32[]{:S(2)}, u32[]{:S(2)}) async-start(f32[64,8,128]{2,1,0:T(8,128)} %get-tuple-element.22), calls=%async_computation | async-start | bytes 524288 | tf_op jit(solution)/shard_map/all_to_all | solution.py:348

commit v3 on v2

v3 whole, which is shorter than its diff:
```python
import jax
import jax.numpy as jnp
from jax import lax
from jax.experimental import pallas as pl
from jax.experimental.pallas import tpu as pltpu
from jax.sharding import PartitionSpec as P

NT = 8
W = 4
SLAB = 8
EXT = SLAB + 2 * W
AX = 64
AY = 128
PAD = 8
ROWS = 16
BODY = slice(PAD, PAD + AX)


def trig(angle):
    square = angle * angle
    sine = -1.0 / 39916800.0
    for term in (1.0 / 362880.0, -1.0 / 5040.0, 1.0 / 120.0, -1.0 / 6.0, 1.0):
        sine = sine * square + term
    cosine = 1.0 / 479001600.0
    for term in (-1.0 / 3628800.0, 1.0 / 40320.0, -1.0 / 720.0, 1.0 / 24.0, -0.5, 1.0):
        cosine = cosine * square + term
    return sine * angle, cosine


def weight_planes(speed, ratio, theta, sweep):
    sine, axis_z = trig(theta)
    half_sine, half_cosine = trig(0.5 * sweep)
    axis_x = sine * (1.0 - 2.0 * half_sine * half_sine)
    axis_y = sine * (2.0 * half_sine * half_cosine)
    tilted = -2.0 * ratio
    base = speed * (1.0 + 2.0 * ratio)
    tilted = speed * tilted
    cross = 0.5 * tilted
    zz = base + tilted * axis_z * axis_z
    xx = base + tilted * axis_x * axis_x
    yy = base + tilted * axis_y * axis_y
    zx = cross * axis_z * axis_x
    zy = cross * axis_z * axis_y
    xy = cross * axis_x * axis_y
    centre = 2.0 - 2.0 * (zz + xx + yy)
    lane = lax.broadcasted_iota(jnp.int32, speed.shape, 1)
    low = lane == 0
    high = lane == AY - 1

    def up(plane):
        return jnp.where(high, 0.0, pltpu.roll(plane, AY - 1, 1))

    def down(plane):
        return jnp.where(low, 0.0, pltpu.roll(plane, 1, 1))

    return (centre, zz, xx, zx, up(yy), up(-zy), up(-xy), down(yy), down(zy), down(xy))


def store_planes(planes, layer, parts, scale):
    for start in range(0, AX, 16):
        part = slice(start, start + 16)
        speed, ratio, theta, sweep = [ref[part].astype(jnp.float32) for ref in parts]
        for index, value in enumerate(weight_planes(speed * scale, ratio, theta, sweep)):
            planes[index, layer - 1, part, :] = value


def loop(first, last, body):
    def step(index, carry):
        body(index)
        return carry

    lax.fori_loop(first, last, step, 0)


def advance(source, target, planes, layer, start):
    part = slice(start, start + ROWS)
    (centre_w, zz, xx, zx, y_low, zy_low, xy_low, y_high, zy_high, xy_high) = [
        planes[i, layer - 1, part, :] for i in range(10)
    ]
    here = slice(PAD + start, PAD + start + ROWS)
    before = slice(PAD + start - 1, PAD + start + ROWS - 1)
    after = slice(PAD + start + 1, PAD + start + ROWS + 1)
    made = []
    for field in range(2):
        centre = source[field, layer, here, :]
        above = source[field, layer + 1, here, :]
        below = source[field, layer - 1, here, :]
        ahead = source[field, layer, after, :]
        behind = source[field, layer, before, :]
        step_z = above - below
        step_x = ahead - behind
        twist = (source[field, layer + 1, after, :] - source[field, layer + 1, before, :]) - (
            source[field, layer - 1, after, :] - source[field, layer - 1, before, :]
        )
        total = centre_w * centre - target[field, layer, here, :]
        total = total + zz * (above + below)
        total = total + xx * (ahead + behind)
        total = total + zx * twist
        total = total + pltpu.roll(y_low * centre + zy_low * step_z + xy_low * step_x, 1, 1)
        total = total + pltpu.roll(y_high * centre + zy_high * step_z + xy_high * step_x, AY - 1, 1)
        target[field, layer, here, :] = total
        made.append(total)
    return made


def advance_halo(source, target, planes, first, last):
    def halo(layer):
        for start in range(0, AX, ROWS):
            advance(source, target, planes, layer, start)

    if last > first:
        loop(first, last, halo)


def advance_own(source, target, planes, picture, fresh):
    def own(layer):
        for start in range(0, AX, ROWS):
            made = advance(source, target, planes, layer + W, start)
            place = pl.ds(pl.multiple_of(layer * AX + start, ROWS), ROWS)
            product = made[0] * made[1]
            picture[place, :] = product if fresh else picture[place, :] + product

    loop(0, SLAB, own)


def pack_kernel(cur, prev, speed, ratio, tilt, azimuth, up_fields, up_media, down_fields, down_media, sems):
    copies = []
    for field in range(2):
        copies.append((cur.at[field, SLAB - W : SLAB], up_fields.at[field, 0:W]))
        copies.append((cur.at[field, 0:W], down_fields.at[field, 0:W]))
        copies.append((prev.at[field, SLAB - W + 1 : SLAB], up_fields.at[field, W : 2 * W - 1]))
        copies.append((prev.at[field, 0 : W - 1], down_fields.at[field, W : 2 * W - 1]))
    for index, part in enumerate((speed, ratio, tilt, azimuth)):
        copies.append((part.at[SLAB - W + 1 : SLAB], up_media.at[index]))
        copies.append((part.at[0 : W - 1], down_media.at[index]))
    started = [pltpu.make_async_copy(a, b, sems.at[i]) for i, (a, b) in enumerate(copies)]
    for copy in started:
        copy.start()
    for copy in started:
        copy.wait()


def own_kernel(cur, prev, speed, ratio, tilt, azimuth, first, second, planes, media, sems):
    own = slice(W, W + SLAB)
    copies = [(part, media.at[index]) for index, part in enumerate((speed, ratio, tilt, azimuth))]
    for field in range(2):
        copies.append((cur.at[field], first.at[field, own, BODY]))
        copies.append((prev.at[field], second.at[field, own, BODY]))
    started = [pltpu.make_async_copy(a, b, sems.at[i]) for i, (a, b) in enumerate(copies)]
    for copy in started:
        copy.start()
    zeros = jnp.zeros((PAD, AY), jnp.float32)

    def clear(layer):
        for field in range(2):
            for buffer in (first, second):
                buffer[field, layer, 0:PAD, :] = zeros
                buffer[field, layer, PAD + AX : PAD + AX + PAD, :] = zeros

    loop(0, EXT, clear)
    for copy in started:
        copy.wait()
    loop(0, SLAB, lambda layer: store_planes(planes, layer + W, [media.at[i, layer] for i in range(4)], 1.0))


def edge_scales():
    place = lax.axis_index("depth")
    last = lax.axis_size("depth") - 1
    return jnp.where(place > 0, 1.0, 0.0), jnp.where(place < last, 1.0, 0.0)


def take_fields(fields, scale, first, second, base, later):
    for field in range(2):
        def take(layer):
            first[field, layer + base, BODY, :] = fields[field, layer] * scale

        def take_other(layer):
            second[field, layer + later, BODY, :] = fields[field, layer + W] * scale

        loop(0, W, take)
        loop(0, W - 1, take_other)


def take_halos(fields_low, fields_high, first, second):
    low, high = edge_scales()
    take_fields(fields_low, low, first, second, 0, 1)
    take_fields(fields_high, high, first, second, W + SLAB, W + SLAB)


def run_steps(first, second, planes, picture, fresh):
    for step in range(1, W + 1):
        source, target = (first, second) if step % 2 else (second, first)
        advance_halo(source, target, planes, step, W)
        advance_own(source, target, planes, picture, fresh and step == 1)
        advance_halo(source, target, planes, W + SLAB, EXT - step)


def early_kernel(
    fields_low, media_low, fields_high, media_high, first_in, second_in, planes_in,
    first, second, planes, picture, up_fields, down_fields,
):
    low, high = edge_scales()

    def halo_planes(layer):
        store_planes(planes, layer + 1, [media_low.at[i, layer] for i in range(4)], low)
        store_planes(planes, layer + W + SLAB, [media_high.at[i, layer] for i in range(4)], high)

    loop(0, W - 1, halo_planes)
    take_halos(fields_low, fields_high, first, second)
    run_steps(first, second, planes, picture, True)
    for field in range(2):
        def pack(layer):
            up_fields[field, layer] = first[field, layer + SLAB, BODY, :]
            down_fields[field, layer] = first[field, layer + W, BODY, :]

        def pack_other(layer):
            up_fields[field, layer + W] = second[field, layer + SLAB + 1, BODY, :]
            down_fields[field, layer + W] = second[field, layer + W, BODY, :]

        loop(0, W, pack)
        loop(0, W - 1, pack_other)


def late_kernel(
    chosen, fields_low, fields_high, first_in, second_in, planes, picture_in,
    first, second, picture, send,
):
    take_halos(fields_low, fields_high, first, second)
    run_steps(first, second, planes, picture, False)
    for entry in range(chosen.shape[0]):
        send[entry] = picture[pl.ds(chosen[entry], SLAB, stride=AX), :]


VM = pl.BlockSpec(memory_space=pltpu.VMEM)
SM = pl.BlockSpec(memory_space=pltpu.SMEM)
HB = pl.BlockSpec(memory_space=pltpu.HBM)
DOUBLINGS = 14
GRANT = 28 << 20


def table_kernel(anchors, blocks, band_width, depth_damp, chosen, place, inverse, stack):
    size = inverse.shape[0]
    shots = anchors.shape[0]
    held = blocks.shape[0] // shots
    my_shot = lax.axis_index("shot")
    my_anchor = anchors[my_shot]

    def two_of(shot):
        taken = jnp.int32(0)
        rows = [jnp.int32(0), jnp.int32(0)]
        slots = [jnp.int32(held), jnp.int32(held)]
        sent = jnp.int32(0)
        for slot in range(held):
            row = blocks[shot * held + slot] - my_anchor
            valid = (row >= 0) & (row < AX)
            for j in range(2):
                rows[j] = jnp.where(valid & (sent == j), row, rows[j])
            sent = sent + valid.astype(jnp.int32)
            row = blocks[my_shot * held + slot] - anchors[shot]
            valid = (row >= 0) & (row < AX)
            for j in range(2):
                slots[j] = jnp.where(valid & (taken == j), slot, slots[j])
            taken = taken + valid.astype(jnp.int32)
        for j in range(2):
            chosen[2 * shot + j] = rows[j]
            place[2 * shot + j] = slots[j]

    loop(0, shots, two_of)

    row = lax.broadcasted_iota(jnp.int32, (size, size), 0)
    column = lax.broadcasted_iota(jnp.int32, (size, size), 1)
    width_row = jnp.broadcast_to(band_width[...].astype(jnp.float32), (size, size))
    reach = jnp.maximum(width_row, width_row.T)
    distance = jnp.abs(row - column).astype(jnp.float32)
    adjacent = jnp.where((distance > 0.0) & (distance <= reach), 1.0, 0.0)
    scale_row = 1.0 / (depth_damp[...] + jnp.sum(adjacent, axis=0, keepdims=True))
    stack[0:size, :] = jnp.where(row == column, 1.0, 0.0)
    stack[size : 2 * size, :] = adjacent * jnp.broadcast_to(scale_row, (size, size)).T

    def double(counter):
        grown = lax.dot_general(
            stack[...], stack[size : 2 * size, :], (((1,), (0,)), ((), ())),
            precision=lax.Precision.HIGHEST, preferred_element_type=jnp.float32,
        )
        stack[0:size, :] = stack[0:size, :] + grown[:size]
        stack[size : 2 * size, :] = grown[size:]

    loop(0, DOUBLINGS, double)
    inverse[...] = stack[0:size, :] * scale_row


def gather_kernel(place, rows_in, out, held):
    for slot in range(held.shape[0]):
        held[slot] = jnp.zeros((SLAB, AY), jnp.float32)
    for entry in range(rows_in.shape[0]):
        slot = place[entry]
        held[slot] = held[slot] + rows_in[entry]
    slots = held.shape[0] - 1
    part = AY // out.shape[0]
    lane = lax.broadcasted_iota(jnp.int32, (SLAB, AY), 1)
    for piece in range(out.shape[0]):
        mixed = None
        for slot in range(slots):
            moved = held[slot]
            turn = (slot * part - piece * part) % AY
            if turn:
                moved = pltpu.roll(moved, turn, 1)
            mixed = moved if mixed is None else jnp.where(lane >= slot * part, moved, mixed)
        out[piece] = mixed * (1.0 / NT)


def apply_kernel(inverse, columns, out):
    solved = lax.dot_general(
        columns[...], inverse[...], (((0,), (1,)), ((), ())),
        precision=lax.Precision.HIGHEST, preferred_element_type=jnp.float32,
    )
    slots, part = out.shape[:2]
    for slot in range(slots):
        out[slot] = solved[slot * part : (slot + 1) * part]


def shards(
    prev_fields, cur_fields, speed_term, epsilon, tilt, azimuth,
    aperture_anchor, slot_block, band_width, depth_damp,
):
    depth = lax.axis_size("depth")
    shots = lax.axis_size("shot")
    held = slot_block.shape[0] // shots
    length = band_width.shape[0]
    upward = [(i, (i + 1) % depth) for i in range(depth)]
    downward = [((i + 1) % depth, i) for i in range(depth)]
    prev, cur = prev_fields[0], cur_fields[0]
    media = [speed_term[0], epsilon[0], tilt[0], azimuth[0]]
    prev, cur, *media = [pltpu.with_memory_space_constraint(x, pltpu.HBM) for x in (prev, cur, *media)]

    def exchange(up, down):
        return lax.ppermute(up, "depth", upward), lax.ppermute(down, "depth", downward)

    def f32(*shape):
        return jax.ShapeDtypeStruct(shape, jnp.float32)

    buffer = f32(2, EXT, AX + 2 * PAD, AY)
    plane = f32(10, EXT - 2, AX, AY)
    edge_fields = f32(2, 2 * W - 1, AX, AY)
    edge_media = jax.ShapeDtypeStruct((4, W - 1, AX, AY), speed_term.dtype)
    table = jax.ShapeDtypeStruct((2 * shots,), jnp.int32)
    grant = pltpu.CompilerParams(vmem_limit_bytes=GRANT)
    up_fields, up_media, down_fields, down_media = pl.pallas_call(
        pack_kernel,
        out_shape=(edge_fields, edge_media, edge_fields, edge_media),
        in_specs=[HB] * 6,
        out_specs=[VM] * 4,
        scratch_shapes=[pltpu.SemaphoreType.DMA((16,))],
        compiler_params=grant,
    )(cur, prev, *media)
    fields_low, fields_high = exchange(up_fields, down_fields)
    media_low, media_high = exchange(up_media, down_media)
    first, second, planes = pl.pallas_call(
        own_kernel,
        out_shape=(buffer, buffer, plane),
        in_specs=[HB] * 6,
        out_specs=[VM] * 3,
        scratch_shapes=[
            pltpu.VMEM((4, SLAB, AX, AY), speed_term.dtype),
            pltpu.SemaphoreType.DMA((8,)),
        ],
        compiler_params=grant,
    )(cur, prev, *media)
    first, second, planes, picture, up_fields, down_fields = pl.pallas_call(
        early_kernel,
        out_shape=(buffer, buffer, plane, f32(SLAB * AX, AY), edge_fields, edge_fields),
        in_specs=[VM] * 7,
        out_specs=[VM] * 6,
        input_output_aliases={4: 0, 5: 1, 6: 2},
        compiler_params=grant,
    )(fields_low, media_low, fields_high, media_high, first, second, planes)
    up_fields, band_row = lax.optimization_barrier((up_fields, band_width[None, :]))
    fields_low, fields_high = exchange(up_fields, down_fields)
    chosen, place, inverse = pl.pallas_call(
        table_kernel,
        out_shape=(table, table, f32(length, length)),
        in_specs=[SM, SM, VM, VM],
        out_specs=[SM, SM, VM],
        scratch_shapes=[pltpu.VMEM((2 * length, length), jnp.float32)],
        compiler_params=grant,
    )(aperture_anchor, slot_block, band_row, depth_damp[None, :])
    send = pl.pallas_call(
        late_kernel,
        out_shape=(buffer, buffer, f32(SLAB * AX, AY), f32(2 * shots, SLAB, AY)),
        in_specs=[SM] + [VM] * 6,
        out_specs=[VM] * 4,
        input_output_aliases={3: 0, 4: 1, 6: 2},
        compiler_params=grant,
    )(chosen, fields_low, fields_high, first, second, planes, picture)[3]
    received = lax.all_to_all(send, "shot", split_axis=0, concat_axis=0, tiled=True)
    part = AY // depth
    pieces = pl.pallas_call(
        gather_kernel,
        out_shape=jax.ShapeDtypeStruct((depth, SLAB, AY), jnp.float32),
        in_specs=[SM, VM],
        out_specs=VM,
        scratch_shapes=[pltpu.VMEM((held + 1, SLAB, AY), jnp.float32)],
        compiler_params=grant,
    )(place, received)
    columns = lax.all_to_all(pieces, "depth", split_axis=0, concat_axis=0, tiled=True)
    return pl.pallas_call(
        apply_kernel,
        out_shape=jax.ShapeDtypeStruct((held, part, AY), jnp.float32),
        in_specs=[VM, VM],
        out_specs=VM,
        compiler_params=grant,
    )(inverse, columns.reshape(AY, AY))


def solution(mesh):
    placed = (
        P("shot", None, "depth", None, None),
        P("shot", None, "depth", None, None),
        P("shot", "depth", None, None),
        P("shot", "depth", None, None),
        P("shot", "depth", None, None),
        P("shot", "depth", None, None),
        P(),
        P(),
        P(),
        P(),
    )
    return jax.shard_map(
        shards, mesh=mesh, in_specs=placed, out_specs=P("shot", "depth", None), check_vma=False
    )
```

time: 107 us -> 78.5 us (0.73)
  blocking collectives: 19.3 us -> 37.8 us
  other arithmetic: 17.8 us -> 0 us
  waiting for transfers between devices: 10 us -> 0.27 us
  local copies, waits for them, and re-layouts: 9.64 us -> 0.02 us
  starting transfers between devices: 23.3 us -> 14.9 us
  Pallas kernels: 26.4 us -> 25.2 us
    all_to_all x0 -> x1, blocking collectives: none -> 20.6 us  [shards(): lax.all_to_all(send, 'shot', split_axis=0, concat_axis=0, tiled=True)]
    all_to_all x1 -> x0, waiting for transfers between devices: 9.99 us -> none  [shards(): lax.all_to_all(send, 'shot', split_axis=0, concat_axis=0, tiled=True)]
    all_to_all x1 -> x0, starting transfers between devices: 7.54 us -> none  [shards(): lax.all_to_all(send, 'shot', split_axis=0, concat_axis=0, tiled=True)]
    another operation x8 -> x0, other arithmetic: 7.04 us -> none  [the longest x4 4.07 us: cut(): return jnp.stack([part[first:last] for part in parts])]
    slice x6 -> x0, local copies, waits for them, and re-layouts: 5.18 us -> none  [the longest x4 3.3 us: cut(): return jnp.stack([part[first:last] for part in parts])]
    concatenate x4 -> x0, other arithmetic: 4.3 us -> none  [fields(): jnp.concatenate([cur[:, cur_first:cur_last], prev[:, prev_first:prev_last...]
    all_to_all x1, blocking collectives: 19.3 us -> 17.1 us  [shards(): lax.all_to_all(pieces, 'depth', split_axis=0, concat_axis=0, tiled=True)]
    convert_element_type x3 -> x0, other arithmetic: 2.03 us -> none  [the longest x2 1.95 us: pick_rows(): order = jnp.cumsum(valid.astype(jnp.int32), axis=1) - 1]
  transfers between devices with their start and end apart: 9 -> 6, of which waited for: 1 -> 1; matrix products, arithmetic and copies ran while one was open for 23% -> 0% of each run, Pallas kernels for 12% -> 11%
where the time goes in v3:
time: 78.5 us; the launch traced here: 78.3 us
  blocking collectives  37.8 us (48%)
  Pallas kernels  25.2 us (32%)
  starting transfers between devices  14.9 us (19%)
    all_to_all x1, blocking collectives, shards(): lax.all_to_all(send, 'shot', split_axis=0, concat_axis=0, tiled=True)  20.6 us
    all_to_all x1, blocking collectives, shards(): lax.all_to_all(pieces, 'depth', split_axis=0, concat_axis=0, tiled=True)  17.1 us
    ppermute x3, starting transfers between devices, exchange(): lax.ppermute(down, 'depth', downward)  12.2 us
    pallas_call x1, Pallas kernels, shards(): pl.pallas_call(early_kernel, out_shape=(buffer, buffer, plane, f32(SLAB *...  6.61 us
    pallas_call x1, Pallas kernels, shards(): pl.pallas_call(late_kernel, out_shape=(buffer, buffer, f32(SLAB * AX, AY)...  6.53 us
    pallas_call x1, Pallas kernels, shards(): pl.pallas_call(table_kernel, out_shape=(table, table, f32(length, length)...  5.9 us
    pallas_call x1, Pallas kernels, shards(): pl.pallas_call(own_kernel, out_shape=(buffer, buffer, plane), in_specs=[H...  2.9 us
    ppermute x3, starting transfers between devices, exchange(): lax.ppermute(up, 'depth', upward)  2.72 us
  transfers between devices with their start and end apart: 6, of which 1 were waited for; matrix products, arithmetic and copies ran while one was open for 0% of the time, Pallas kernels for 11%

profile of v3, /device:TPU:1, one launch (start us, length us, event | category | flops | bytes accessed | tf_op | source)
XLA Modules:
  0.0 78.3 jit_solution(5180053917929087248)
XLA Ops:
  0.0 1.4 %shard_map.100 = (f32[2,7,64,128]{3,2,1,0:T(8,128)S(1)}, bf16[4,3,64,128]{3,2,1,0:T(8,128)(2,1)S(1)}, f32[2,7,64,128]{3,2,1,0:T(8,128)S(1)}, bf16[4,3,64,128]{3,2,1,0:T(8,128)(2,1)S(1)}) custom-call(f32[2,8,64,128]{3,2,1,0:T(8,128)} %bitcast.12, f32[2,8,64,128]{3,2,1,0:T(8,128)} %bitcast.14, bf16[8,64,128]{2,1,0:T(8,128)(2,1)} %bitcast.16, ...), custom_call_target="tpu_custom_call" | custom-call | tf_op jit(solution)/shard_map/pallas_call | solution.py:348
  1.4 2.7 %collective-permute-start = (f32[2,7,64,128]{3,2,1,0:T(8,128)S(1)}, f32[2,7,64,128]{3,2,1,0:T(8,128)S(1)}, u32[]{:S(2)}, u32[]{:S(2)}) collective-permute-start(f32[2,7,64,128]{3,2,1,0:T(8,128)S(1)} %get-tuple-element.24), channel_id=1, source_target_pairs={{0,1},{1,2},{2,3},{3,4},{4,5},{5,6},{6,7},{7,8},{8,9},{9,10},{10,1... | collective-permute-start | bytes 1376264 | tf_op jit(solution)/shard_map/ppermute | solution.py:337
  4.1 4.2 %collective-permute-start.2 = (f32[2,7,64,128]{3,2,1,0:T(8,128)S(1)}, f32[2,7,64,128]{3,2,1,0:T(8,128)S(1)}, u32[]{:S(2)}, u32[]{:S(2)}) collective-permute-start(f32[2,7,64,128]{3,2,1,0:T(8,128)S(1)} %get-tuple-element.26), channel_id=1, source_target_pairs={{1,0},{2,1},{3,2},{4,3},{5,4},{6,5},{7,6},{8,7},{9,8},{10,9},{11,1... | collective-permute-start | bytes 1376264 | tf_op jit(solution)/shard_map/ppermute | solution.py:337
  8.3 0.0 collective-permute-start.1
  8.3 2.9 %collective-permute-start.3 = (bf16[4,3,64,128]{3,2,1,0:T(8,128)(2,1)S(1)}, bf16[4,3,64,128]{3,2,1,0:T(8,128)(2,1)S(1)}, u32[]{:S(2)}, u32[]{:S(2)}) collective-permute-start(bf16[4,3,64,128]{3,2,1,0:T(8,128)(2,1)S(1)} %get-tuple-element.27), channel_id=1, source_target_pairs={{1,0},{2,1},{3,2},{4,3},{5,4},{6,5},{7,6},{8,7},{9,8},{10,9},{11,1... | collective-permute-start | bytes 589832 | tf_op jit(solution)/shard_map/ppermute | solution.py:337
  11.2 2.9 %shard_map.101 = (f32[2,16,80,128]{3,2,1,0:T(8,128)S(1)}, f32[2,16,80,128]{3,2,1,0:T(8,128)S(1)}, f32[10,14,64,128]{3,2,1,0:T(8,128)S(1)}) custom-call(f32[2,8,64,128]{3,2,1,0:T(8,128)} %bitcast.13, f32[2,8,64,128]{3,2,1,0:T(8,128)} %bitcast.15, bf16[8,64,128]{2,1,0:T(8,128)(2,1)} %bitcast.17, bf16[8,64,128]{2,1,0:T(8,128)(2,1)} %bitcast.19, ...), custom_call_target="tpu_custom_call" | custom-call | tf_op jit(solution)/shard_map/pallas_call | solution.py:358
  14.2 0.0 collective-permute-done.1.media_low
  14.2 0.3 collective-permute-done.3.media_high
  14.4 0.0 collective-permute-done.fields_low
  14.4 0.0 collective-permute-done.2.fields_high
  14.4 0.0 copy-start
  14.4 0.0 copy-start.1
  14.4 0.0 copy-start.2
  14.5 0.0 copy-start.3
  14.5 6.6 %shard_map.102 = (f32[2,16,80,128]{3,2,1,0:T(8,128)S(1)}, f32[2,16,80,128]{3,2,1,0:T(8,128)S(1)}, f32[10,14,64,128]{3,2,1,0:T(8,128)S(1)}, f32[512,128]{1,0:T(8,...) custom-call(f32[2,7,64,128]{3,2,1,0:T(8,128)S(1)} %collective-permut, ...), custom_call_target="tpu_custom_call", output_to_operand_aliasing={{0}: (4, {}), {1}: (5, {}), {2}: (6, {})} | custom-call | tf_op jit(solution)/shard_map/pallas_call | solution.py:369
  21.1 0.0 collective-permute-start.4
  21.1 5.1 %collective-permute-start.5 = (f32[2,7,64,128]{3,2,1,0:T(8,128)S(1)}, f32[2,7,64,128]{3,2,1,0:T(8,128)S(1)}, u32[]{:S(2)}, u32[]{:S(2)}) collective-permute-start(f32[2,7,64,128]{3,2,1,0:T(8,128)S(1)} %get-tuple-element.37), channel_id=1, source_target_pairs={{1,0},{2,1},{3,2},{4,3},{5,4},{6,5},{7,6},{8,7},{9,8},{10,9},{11,1... | collective-permute-start | bytes 1376264 | tf_op jit(solution)/shard_map/ppermute | solution.py:337
  26.2 0.0 copy-done
  26.2 0.0 copy-done.1
  26.2 0.0 copy-done.2
  26.2 0.0 copy-done.3
  26.2 5.9 %shard_map.103 = (s32[64]{0:T(128)S(1)}, s32[64]{0:T(128)S(1)}, f32[128,128]{1,0:T(8,128)S(1)}) custom-call(s32[32]{0:T(128)S(1)} %copy-done, s32[128]{0:T(128)S(1)} %copy-done.1, s32[1,128]{1,0:T(1,128)S(1)} %bitcast.10, f32[1,128]{1,0:T(1,128)S(1)} %bitcast.11), custom_call_target="tpu_custom_call" | custom-call | tf_op jit(solution)/shard_map/pallas_call | solution.py:379
  32.1 0.0 collective-permute-done.4.fields_low
  32.1 0.0 collective-permute-done.5.fields_high
  32.2 6.5 %shard_map.104 = (f32[2,16,80,128]{3,2,1,0:T(8,128)S(1)}, f32[2,16,80,128]{3,2,1,0:T(8,128)S(1)}, f32[512,128]{1,0:T(8,128)S(1)}, f32[64,8,128]{2,1,0:T(8,128)S(1)}) custom-call(s32[64]{0:T(128)S(1)} %get-tuple-element.35.chosen, f32[2,7,64,128]{3,2,1,0:T(8,128)S(1)} %collective-permute-done.4.fields_low, ...), custom_call_target="tpu_custom_call", output_to_operand_aliasing={{0}: (3, {}), {1}: (4, {}), {2}: (6, {})} | custom-call | tf_op jit(solution)/shard_map/pallas_call | solution.py:387
  38.7 20.6 %all_to_all.10.rows_in = f32[64,8,128]{2,1,0:T(8,128)S(1)} all-to-all(f32[64,8,128]{2,1,0:T(8,128)S(1)} %get-tuple-element.42), channel_id=1, replica_groups=mesh['shot'=32,'depth'=16] {'shot'}, dimensions={0} | all-to-all | bytes 524288 | tf_op jit(solution)/shard_map/all_to_all | solution.py:395
  59.3 0.9 %shard_map.105 = f32[16,8,128]{2,1,0:T(8,128)S(1)} custom-call(s32[64]{0:T(128)S(1)} %get-tuple-element.34.place, f32[64,8,128]{2,1,0:T(8,128)S(1)} %all_to_all.10.rows_in), custom_call_target="tpu_custom_call" | custom-call | tf_op jit(solution)/shard_map/pallas_call | solution.py:397
  60.3 17.1 %all_to_all.11 = f32[16,8,128]{2,1,0:T(8,128)S(1)} all-to-all(f32[16,8,128]{2,1,0:T(8,128)S(1)} %shard_map.105), channel_id=1, replica_groups=mesh['shot'=32,'depth'=16] {'depth'}, dimensions={0} | all-to-all | bytes 131072 | tf_op jit(solution)/shard_map/all_to_all | solution.py:405
  77.4 0.9 %shard_map.106 = f32[4,8,128]{2,1,0:T(8,128)} custom-call(f32[128,128]{1,0:T(8,128)S(1)} %get-tuple-element.33.inverse, f32[128,128]{1,0:T(8,128)S(1)} %bitcast.9), custom_call_target="tpu_custom_call" | custom-call | tf_op jit(solution)/shard_map/pallas_call | solution.py:406
Async XLA Ops:
  1.4 13.0 %collective-permute-start = (f32[2,7,64,128]{3,2,1,0:T(8,128)S(1)}, f32[2,7,64,128]{3,2,1,0:T(8,128)S(1)}, u32[]{:S(2)}, u32[]{:S(2)}) collective-permute-start(f32[2,7,64,128]{3,2,1,0:T(8,128)S(1)} %get-tuple-element.24), channel_id=1, source_target_pairs={{0,1},{1,2},{2,3},{3,4},{4,5},{5,6},{6,7},{7,8},{8,9},{9,10},{10,1... | collective-permute-start | bytes 1376264 | tf_op jit(solution)/shard_map/ppermute | solution.py:337
  4.1 10.3 %collective-permute-start.2 = (f32[2,7,64,128]{3,2,1,0:T(8,128)S(1)}, f32[2,7,64,128]{3,2,1,0:T(8,128)S(1)}, u32[]{:S(2)}, u32[]{:S(2)}) collective-permute-start(f32[2,7,64,128]{3,2,1,0:T(8,128)S(1)} %get-tuple-element.26), channel_id=1, source_target_pairs={{1,0},{2,1},{3,2},{4,3},{5,4},{6,5},{7,6},{8,7},{9,8},{10,9},{11,1... | collective-permute-start | bytes 1376264 | tf_op jit(solution)/shard_map/ppermute | solution.py:337
  8.3 5.8 %collective-permute-start.1 = (bf16[4,3,64,128]{3,2,1,0:T(8,128)(2,1)S(1)}, bf16[4,3,64,128]{3,2,1,0:T(8,128)(2,1)S(1)}, u32[]{:S(2)}, u32[]{:S(2)}) collective-permute-start(bf16[4,3,64,128]{3,2,1,0:T(8,128)(2,1)S(1)} %get-tuple-element.25), channel_id=1, source_target_pairs={{0,1},{1,2},{2,3},{3,4},{4,5},{5,6},{6,7},{7,8},{8,9},{9,10},{10,1... | collective-permute-start | bytes 589832 | tf_op jit(solution)/shard_map/ppermute | solution.py:337
  8.3 6.1 %collective-permute-start.3 = (bf16[4,3,64,128]{3,2,1,0:T(8,128)(2,1)S(1)}, bf16[4,3,64,128]{3,2,1,0:T(8,128)(2,1)S(1)}, u32[]{:S(2)}, u32[]{:S(2)}) collective-permute-start(bf16[4,3,64,128]{3,2,1,0:T(8,128)(2,1)S(1)} %get-tuple-element.27), channel_id=1, source_target_pairs={{1,0},{2,1},{3,2},{4,3},{5,4},{6,5},{7,6},{8,7},{9,8},{10,9},{11,1... | collective-permute-start | bytes 589832 | tf_op jit(solution)/shard_map/ppermute | solution.py:337
  14.4 11.8 %copy-start = (s32[32]{0:T(128)S(1)}, s32[32]{0:T(128)}, u32[]{:S(2)}) copy-start(s32[32]{0:T(128)} %anchors.1) | copy-start | bytes 388
  14.4 11.8 %copy-start.1 = (s32[128]{0:T(128)S(1)}, s32[128]{0:T(128)}, u32[]{:S(2)}) copy-start(s32[128]{0:T(128)} %blocks.1) | copy-start | bytes 1540
  14.4 11.8 %copy-start.2 = (s32[128]{0:T(128)S(1)}, s32[128]{0:T(128)}, u32[]{:S(2)}) copy-start(s32[128]{0:T(128)} %param.18) | copy-start | bytes 1540
  14.5 11.8 %copy-start.3 = (f32[128]{0:T(128)S(1)}, f32[128]{0:T(128)}, u32[]{:S(2)}) copy-start(f32[128]{0:T(128)} %param.19) | copy-start | bytes 1540
  21.1 11.1 %collective-permute-start.4 = (f32[2,7,64,128]{3,2,1,0:T(8,128)S(1)}, f32[2,7,64,128]{3,2,1,0:T(8,128)S(1)}, u32[]{:S(2)}, u32[]{:S(2)}) collective-permute-start(f32[2,7,64,128]{3,2,1,0:T(8,128)S(1)} %get-tuple-element.36), channel_id=1, source_target_pairs={{0,1},{1,2},{2,3},{3,4},{4,5},{5,6},{6,7},{7,8},{8,9},{9,10},{10,1... | collective-permute-start | bytes 1376264 | tf_op jit(solution)/shard_map/ppermute | solution.py:337
  21.1 11.0 %collective-permute-start.5 = (f32[2,7,64,128]{3,2,1,0:T(8,128)S(1)}, f32[2,7,64,128]{3,2,1,0:T(8,128)S(1)}, u32[]{:S(2)}, u32[]{:S(2)}) collective-permute-start(f32[2,7,64,128]{3,2,1,0:T(8,128)S(1)} %get-tuple-element.37), channel_id=1, source_target_pairs={{1,0},{2,1},{3,2},{4,3},{5,4},{6,5},{7,6},{8,7},{9,8},{10,9},{11,1... | collective-permute-start | bytes 1376264 | tf_op jit(solution)/shard_map/ppermute | solution.py:337

commit v4 on v3

--- a/solution.py
+++ b/solution.py
@@ -103,24 +103,16 @@
     return made
 
 
-def advance_halo(source, target, planes, first, last):
-    def halo(layer):
+def advance_layers(source, target, planes, picture, first_layer, last_layer):
+    def at(layer, own):
         for start in range(0, AX, ROWS):
-            advance(source, target, planes, layer, start)
-
-    if last > first:
-        loop(first, last, halo)
-
-
-def advance_own(source, target, planes, picture, fresh):
-    def own(layer):
-        for start in range(0, AX, ROWS):
-            made = advance(source, target, planes, layer + W, start)
-            place = pl.ds(pl.multiple_of(layer * AX + start, ROWS), ROWS)
-            product = made[0] * made[1]
-            picture[place, :] = product if fresh else picture[place, :] + product
-
-    loop(0, SLAB, own)
+            made = advance(source, target, planes, layer, start)
+            if own:
+                place = pl.ds((layer - W) * AX + start, ROWS)
+                picture[place, :] = picture[place, :] + made[0] * made[1]
+
+    for layer in range(first_layer, last_layer):
+        at(layer, W <= layer < W + SLAB)
 
 
 def pack_kernel(cur, prev, speed, ratio, tilt, azimuth, up_fields, up_media, down_fields, down_media, sems):
@@ -140,7 +132,7 @@
         copy.wait()
 
 
-def own_kernel(cur, prev, speed, ratio, tilt, azimuth, first, second, planes, media, sems):
+def own_kernel(cur, prev, speed, ratio, tilt, azimuth, first, second, planes, picture, media, sems):
     own = slice(W, W + SLAB)
     copies = [(part, media.at[index]) for index, part in enumerate((speed, ratio, tilt, azimuth))]
     for field in range(2):
@@ -158,9 +150,11 @@
                 buffer[field, layer, PAD + AX : PAD + AX + PAD, :] = zeros
 
     loop(0, EXT, clear)
+    picture[...] = jnp.zeros_like(picture)
     for copy in started:
         copy.wait()
     loop(0, SLAB, lambda layer: store_planes(planes, layer + W, [media.at[i, layer] for i in range(4)], 1.0))
+    inner_steps(first, second, planes, picture)
 
 
 def edge_scales():
@@ -187,16 +181,21 @@
     take_fields(fields_high, high, first, second, W + SLAB, W + SLAB)
 
 
-def run_steps(first, second, planes, picture, fresh):
+def inner_steps(first, second, planes, picture):
+    for step in range(1, W):
+        source, target = (first, second) if step % 2 else (second, first)
+        advance_layers(source, target, planes, picture, W + step, W + SLAB - step)
+
+
+def outer_steps(first, second, planes, picture):
     for step in range(1, W + 1):
         source, target = (first, second) if step % 2 else (second, first)
-        advance_halo(source, target, planes, step, W)
-        advance_own(source, target, planes, picture, fresh and step == 1)
-        advance_halo(source, target, planes, W + SLAB, EXT - step)
+        advance_layers(source, target, planes, picture, step, W + step)
+        advance_layers(source, target, planes, picture, W + SLAB - step, EXT - step)
 
 
 def early_kernel(
-    fields_low, media_low, fields_high, media_high, first_in, second_in, planes_in,
+    fields_low, media_low, fields_high, media_high, first_in, second_in, planes_in, picture_in,
     first, second, planes, picture, up_fields, down_fields,
 ):
     low, high = edge_scales()
@@ -207,7 +206,7 @@
 
     loop(0, W - 1, halo_planes)
     take_halos(fields_low, fields_high, first, second)
-    run_steps(first, second, planes, picture, True)
+    outer_steps(first, second, planes, picture)
     for field in range(2):
         def pack(layer):
             up_fields[field, layer] = first[field, layer + SLAB, BODY, :]
@@ -219,6 +218,10 @@
 
         loop(0, W, pack)
         loop(0, W - 1, pack_other)
+
+
+def between_kernel(first_in, second_in, planes, picture_in, first, second, picture):
+    inner_steps(first, second, planes, picture)
 
 
 def late_kernel(
@@ -226,7 +229,7 @@
     first, second, picture, send,
 ):
     take_halos(fields_low, fields_high, first, second)
-    run_steps(first, second, planes, picture, False)
+    outer_steps(first, second, planes, picture)
     for entry in range(chosen.shape[0]):
         send[entry] = picture[pl.ds(chosen[entry], SLAB, stride=AX), :]
 
@@ -234,7 +237,7 @@
 VM = pl.BlockSpec(memory_space=pltpu.VMEM)
 SM = pl.BlockSpec(memory_space=pltpu.SMEM)
 HB = pl.BlockSpec(memory_space=pltpu.HBM)
-DOUBLINGS = 14
+DOUBLINGS = 13
 GRANT = 28 << 20
 
 
@@ -355,11 +358,12 @@
     )(cur, prev, *media)
     fields_low, fields_high = exchange(up_fields, down_fields)
     media_low, media_high = exchange(up_media, down_media)
-    first, second, planes = pl.pallas_call(
+    image = f32(SLAB * AX, AY)
+    first, second, planes, picture = pl.pallas_call(
         own_kernel,
-        out_shape=(buffer, buffer, plane),
+        out_shape=(buffer, buffer, plane, image),
         in_specs=[HB] * 6,
-        out_specs=[VM] * 3,
+        out_specs=[VM] * 4,
         scratch_shapes=[
             pltpu.VMEM((4, SLAB, AX, AY), speed_term.dtype),
             pltpu.SemaphoreType.DMA((8,)),
@@ -368,12 +372,12 @@
     )(cur, prev, *media)
     first, second, planes, picture, up_fields, down_fields = pl.pallas_call(
         early_kernel,
-        out_shape=(buffer, buffer, plane, f32(SLAB * AX, AY), edge_fields, edge_fields),
-        in_specs=[VM] * 7,
+        out_shape=(buffer, buffer, plane, image, edge_fields, edge_fields),
+        in_specs=[VM] * 8,
         out_specs=[VM] * 6,
-        input_output_aliases={4: 0, 5: 1, 6: 2},
-        compiler_params=grant,
-    )(fields_low, media_low, fields_high, media_high, first, second, planes)
+        input_output_aliases={4: 0, 5: 1, 6: 2, 7: 3},
+        compiler_params=grant,
+    )(fields_low, media_low, fields_high, media_high, first, second, planes, picture)
     up_fields, band_row = lax.optimization_barrier((up_fields, band_width[None, :]))
     fields_low, fields_high = exchange(up_fields, down_fields)
     chosen, place, inverse = pl.pallas_call(
@@ -384,9 +388,17 @@
         scratch_shapes=[pltpu.VMEM((2 * length, length), jnp.float32)],
         compiler_params=grant,
     )(aperture_anchor, slot_block, band_row, depth_damp[None, :])
+    first, second, picture = pl.pallas_call(
+        between_kernel,
+        out_shape=(buffer, buffer, image),
+        in_specs=[VM] * 4,
+        out_specs=[VM] * 3,
+        input_output_aliases={0: 0, 1: 1, 3: 2},
+        compiler_params=grant,
+    )(first, second, planes, picture)
     send = pl.pallas_call(
         late_kernel,
-        out_shape=(buffer, buffer, f32(SLAB * AX, AY), f32(2 * shots, SLAB, AY)),
+        out_shape=(buffer, buffer, image, f32(2 * shots, SLAB, AY)),
         in_specs=[SM] + [VM] * 6,
         out_specs=[VM] * 4,
         input_output_aliases={3: 0, 4: 1, 6: 2},

time: 78.5 us -> 72.7 us (0.926)
  Pallas kernels: 25.2 us -> 21.2 us
  starting transfers between devices: 14.9 us -> 14.1 us
  blocking collectives: 37.8 us -> 37 us
    pallas_call x3 -> x4, Pallas kernels: 16 us -> 12.4 us  [the longest x1 3.94 us: shards(): pl.pallas_call(own_kernel, out_shape=(buffer, buffer, plane, image), in_s...]
    all_to_all x1, blocking collectives: 20.6 us -> 19.2 us  [shards(): lax.all_to_all(send, 'shot', split_axis=0, concat_axis=0, tiled=True)]
    ppermute x3, starting transfers between devices: 12.2 us -> 11.4 us  [exchange(): lax.ppermute(down, 'depth', downward)]
  transfers between devices with their start and end apart: 6 -> 6, of which waited for: 1 -> 0; matrix products, arithmetic and copies ran while one was open for 0% -> 0% of each run, Pallas kernels for 11% -> 15%
where the time goes in v4:
time: 72.7 us; the launch traced here: 72.5 us
  blocking collectives  37 us (51%)
  Pallas kernels  21.2 us (29%)
  starting transfers between devices  14.1 us (19%)
    all_to_all x1, blocking collectives, shards(): lax.all_to_all(send, 'shot', split_axis=0, concat_axis=0, tiled=True)  19.2 us
    all_to_all x1, blocking collectives, shards(): lax.all_to_all(pieces, 'depth', split_axis=0, concat_axis=0, tiled=True)  17.8 us
    ppermute x3, starting transfers between devices, exchange(): lax.ppermute(down, 'depth', downward)  11.4 us
    pallas_call x1, Pallas kernels, shards(): pl.pallas_call(table_kernel, out_shape=(table, table, f32(length, length)...  5.64 us
    pallas_call x1, Pallas kernels, shards(): pl.pallas_call(own_kernel, out_shape=(buffer, buffer, plane, image), in_s...  3.94 us
    pallas_call x1, Pallas kernels, shards(): pl.pallas_call(early_kernel, out_shape=(buffer, buffer, plane, image, edg...  3.73 us
    pallas_call x1, Pallas kernels, shards(): pl.pallas_call(late_kernel, out_shape=(buffer, buffer, image, f32(2 * sho...  3.66 us
    ppermute x3, starting transfers between devices, exchange(): lax.ppermute(up, 'depth', upward)  2.71 us
  transfers between devices with their start and end apart: 6, of which 0 were waited for; matrix products, arithmetic and copies ran while one was open for 0% of the time, Pallas kernels for 15%

profile of v4, /device:TPU:1, one launch (start us, length us, event | category | flops | bytes accessed | tf_op | source)
XLA Modules:
  0.0 72.5 jit_solution(6747909667521755113)
XLA Ops:
  0.0 1.4 %shard_map.100 = (f32[2,7,64,128]{3,2,1,0:T(8,128)S(1)}, bf16[4,3,64,128]{3,2,1,0:T(8,128)(2,1)S(1)}, f32[2,7,64,128]{3,2,1,0:T(8,128)S(1)}, bf16[4,3,64,128]{3,2,1,0:T(8,128)(2,1)S(1)}) custom-call(f32[2,8,64,128]{3,2,1,0:T(8,128)} %bitcast.12, f32[2,8,64,128]{3,2,1,0:T(8,128)} %bitcast.14, bf16[8,64,128]{2,1,0:T(8,128)(2,1)} %bitcast.16, ...), custom_call_target="tpu_custom_call" | custom-call | tf_op jit(solution)/shard_map/pallas_call | solution.py:351
  1.4 2.7 %collective-permute-start = (f32[2,7,64,128]{3,2,1,0:T(8,128)S(1)}, f32[2,7,64,128]{3,2,1,0:T(8,128)S(1)}, u32[]{:S(2)}, u32[]{:S(2)}) collective-permute-start(f32[2,7,64,128]{3,2,1,0:T(8,128)S(1)} %get-tuple-element.28), channel_id=1, source_target_pairs={{0,1},{1,2},{2,3},{3,4},{4,5},{5,6},{6,7},{7,8},{8,9},{9,10},{10,1... | collective-permute-start | bytes 1376264 | tf_op jit(solution)/shard_map/ppermute | solution.py:340
  4.1 4.2 %collective-permute-start.2 = (f32[2,7,64,128]{3,2,1,0:T(8,128)S(1)}, f32[2,7,64,128]{3,2,1,0:T(8,128)S(1)}, u32[]{:S(2)}, u32[]{:S(2)}) collective-permute-start(f32[2,7,64,128]{3,2,1,0:T(8,128)S(1)} %get-tuple-element.30), channel_id=1, source_target_pairs={{1,0},{2,1},{3,2},{4,3},{5,4},{6,5},{7,6},{8,7},{9,8},{10,9},{11,1... | collective-permute-start | bytes 1376264 | tf_op jit(solution)/shard_map/ppermute | solution.py:340
  8.3 0.0 collective-permute-start.1
  8.3 2.9 %collective-permute-start.3 = (bf16[4,3,64,128]{3,2,1,0:T(8,128)(2,1)S(1)}, bf16[4,3,64,128]{3,2,1,0:T(8,128)(2,1)S(1)}, u32[]{:S(2)}, u32[]{:S(2)}) collective-permute-start(bf16[4,3,64,128]{3,2,1,0:T(8,128)(2,1)S(1)} %get-tuple-element.31), channel_id=1, source_target_pairs={{1,0},{2,1},{3,2},{4,3},{5,4},{6,5},{7,6},{8,7},{9,8},{10,9},{11,1... | collective-permute-start | bytes 589832 | tf_op jit(solution)/shard_map/ppermute | solution.py:340
  11.2 3.9 %shard_map.101 = (f32[2,16,80,128]{3,2,1,0:T(8,128)S(1)}, f32[2,16,80,128]{3,2,1,0:T(8,128)S(1)}, f32[10,14,64,128]{3,2,1,0:T(8,128)S(1)}, f32[512,128]{1,0:T(8,128)S(1)}) custom-call(f32[2,8,64,128]{3,2,1,0:T(8,128)} %bitcast.13, f32[2,8,64,128]{3,2,1,0:T(8,128)} %bitcast.15, bf16[8,64,128]{2,1,0:T(8,128)(2,1)} %bitcast.17, bf16[8,64,128]{2,1,0:T(8,128)(2,1)} %bitcast.19, ...), custom_call_target="tpu_custom_call" | custom-call | tf_op jit(solution)/shard_map/pallas_call | solution.py:362
  15.2 0.0 collective-permute-done.1.media_low
  15.2 0.0 collective-permute-done.3.media_high
  15.2 0.0 collective-permute-done.fields_low
  15.2 0.0 collective-permute-done.2.fields_high
  15.2 0.0 copy-start
  15.2 0.0 copy-start.1
  15.3 0.0 copy-start.2
  15.3 0.0 copy-start.3
  15.3 3.7 %shard_map.102 = (f32[2,16,80,128]{3,2,1,0:T(8,128)S(1)}, f32[2,16,80,128]{3,2,1,0:T(8,128)S(1)}, f32[10,14,64,128]{3,2,1,0:T(8,128)S(1)}, f32[512,128]{1,0:T(8,...) custom-call(f32[2,7,64,128]{3,2,1,0:T(8,128)S(1)} %collective-permut, ...), custom_call_target="tpu_custom_call", output_to_operand_aliasing={{0}: (4, {}), {1}: (5, {}), {2}: (6, {}), {3}: (7, {})} | custom-call | tf_op jit(solution)/shard_map/pallas_call | solution.py:373
  19.0 0.0 collective-permute-start.4
  19.0 4.3 %collective-permute-start.5 = (f32[2,7,64,128]{3,2,1,0:T(8,128)S(1)}, f32[2,7,64,128]{3,2,1,0:T(8,128)S(1)}, u32[]{:S(2)}, u32[]{:S(2)}) collective-permute-start(f32[2,7,64,128]{3,2,1,0:T(8,128)S(1)} %get-tuple-element.42), channel_id=1, source_target_pairs={{1,0},{2,1},{3,2},{4,3},{5,4},{6,5},{7,6},{8,7},{9,8},{10,9},{11,1... | collective-permute-start | bytes 1376264 | tf_op jit(solution)/shard_map/ppermute | solution.py:340
  23.3 0.0 copy-done
  23.3 0.0 copy-done.1
  23.3 0.0 copy-done.2
  23.3 0.0 copy-done.3
  23.4 5.6 %shard_map.103 = (s32[64]{0:T(128)S(1)}, s32[64]{0:T(128)S(1)}, f32[128,128]{1,0:T(8,128)S(1)}) custom-call(s32[32]{0:T(128)S(1)} %copy-done, s32[128]{0:T(128)S(1)} %copy-done.1, s32[1,128]{1,0:T(1,128)S(1)} %bitcast.10, f32[1,128]{1,0:T(1,128)S(1)} %bitcast.11), custom_call_target="tpu_custom_call" | custom-call | tf_op jit(solution)/shard_map/pallas_call | solution.py:383
  29.0 1.0 %shard_map.104 = (f32[2,16,80,128]{3,2,1,0:T(8,128)S(1)}, f32[2,16,80,128]{3,2,1,0:T(8,128)S(1)}, f32[512,128]{1,0:T(8,128)S(1)}) custom-call(f32[2,16,80,128]{3,2,1,0:T(8,128)S(1)} %get-tuple-element.43.first_in, f32[2,16,80,128]{3,2,1,0:T(8,128)S(1)} %get-tuple-element.44.second_in, ...), custom_call_target="tpu_custom_call", output_to_operand_aliasing={{0}: (0, {}), {1}: (1, {}), {2}: (3, {})} | custom-call | tf_op jit(solution)/shard_map/pallas_call | solution.py:391
  30.0 0.0 collective-permute-done.4.fields_low
  30.1 0.0 collective-permute-done.5.fields_high
  30.1 3.7 %shard_map.105 = (f32[2,16,80,128]{3,2,1,0:T(8,128)S(1)}, f32[2,16,80,128]{3,2,1,0:T(8,128)S(1)}, f32[512,128]{1,0:T(8,128)S(1)}, f32[64,8,128]{2,1,0:T(8,128)S(1)}) custom-call(s32[64]{0:T(128)S(1)} %get-tuple-element.40.chosen, f32[2,7,64,128]{3,2,1,0:T(8,128)S(1)} %collective-permute-done.4.fields_low, ...), custom_call_target="tpu_custom_call", output_to_operand_aliasing={{0}: (3, {}), {1}: (4, {}), {2}: (6, {})} | custom-call | tf_op jit(solution)/shard_map/pallas_call | solution.py:399
  33.7 19.2 %all_to_all.10.rows_in = f32[64,8,128]{2,1,0:T(8,128)S(1)} all-to-all(f32[64,8,128]{2,1,0:T(8,128)S(1)} %get-tuple-element.50), channel_id=1, replica_groups=mesh['shot'=32,'depth'=16] {'shot'}, dimensions={0} | all-to-all | bytes 524288 | tf_op jit(solution)/shard_map/all_to_all | solution.py:407
  52.9 1.0 %shard_map.106 = f32[16,8,128]{2,1,0:T(8,128)S(1)} custom-call(s32[64]{0:T(128)S(1)} %get-tuple-element.39.place, f32[64,8,128]{2,1,0:T(8,128)S(1)} %all_to_all.10.rows_in), custom_call_target="tpu_custom_call" | custom-call | tf_op jit(solution)/shard_map/pallas_call | solution.py:409
  53.9 17.8 %all_to_all.11 = f32[16,8,128]{2,1,0:T(8,128)S(1)} all-to-all(f32[16,8,128]{2,1,0:T(8,128)S(1)} %shard_map.106), channel_id=1, replica_groups=mesh['shot'=32,'depth'=16] {'depth'}, dimensions={0} | all-to-all | bytes 131072 | tf_op jit(solution)/shard_map/all_to_all | solution.py:417
  71.7 0.9 %shard_map.107 = f32[4,8,128]{2,1,0:T(8,128)} custom-call(f32[128,128]{1,0:T(8,128)S(1)} %get-tuple-element.38.inverse, f32[128,128]{1,0:T(8,128)S(1)} %bitcast.9), custom_call_target="tpu_custom_call" | custom-call | tf_op jit(solution)/shard_map/pallas_call | solution.py:418
Async XLA Ops:
  1.4 13.8 %collective-permute-start = (f32[2,7,64,128]{3,2,1,0:T(8,128)S(1)}, f32[2,7,64,128]{3,2,1,0:T(8,128)S(1)}, u32[]{:S(2)}, u32[]{:S(2)}) collective-permute-start(f32[2,7,64,128]{3,2,1,0:T(8,128)S(1)} %get-tuple-element.28), channel_id=1, source_target_pairs={{0,1},{1,2},{2,3},{3,4},{4,5},{5,6},{6,7},{7,8},{8,9},{9,10},{10,1... | collective-permute-start | bytes 1376264 | tf_op jit(solution)/shard_map/ppermute | solution.py:340
  4.1 11.1 %collective-permute-start.2 = (f32[2,7,64,128]{3,2,1,0:T(8,128)S(1)}, f32[2,7,64,128]{3,2,1,0:T(8,128)S(1)}, u32[]{:S(2)}, u32[]{:S(2)}) collective-permute-start(f32[2,7,64,128]{3,2,1,0:T(8,128)S(1)} %get-tuple-element.30), channel_id=1, source_target_pairs={{1,0},{2,1},{3,2},{4,3},{5,4},{6,5},{7,6},{8,7},{9,8},{10,9},{11,1... | collective-permute-start | bytes 1376264 | tf_op jit(solution)/shard_map/ppermute | solution.py:340
  8.3 6.9 %collective-permute-start.1 = (bf16[4,3,64,128]{3,2,1,0:T(8,128)(2,1)S(1)}, bf16[4,3,64,128]{3,2,1,0:T(8,128)(2,1)S(1)}, u32[]{:S(2)}, u32[]{:S(2)}) collective-permute-start(bf16[4,3,64,128]{3,2,1,0:T(8,128)(2,1)S(1)} %get-tuple-element.29), channel_id=1, source_target_pairs={{0,1},{1,2},{2,3},{3,4},{4,5},{5,6},{6,7},{7,8},{8,9},{9,10},{10,1... | collective-permute-start | bytes 589832 | tf_op jit(solution)/shard_map/ppermute | solution.py:340
  8.3 6.9 %collective-permute-start.3 = (bf16[4,3,64,128]{3,2,1,0:T(8,128)(2,1)S(1)}, bf16[4,3,64,128]{3,2,1,0:T(8,128)(2,1)S(1)}, u32[]{:S(2)}, u32[]{:S(2)}) collective-permute-start(bf16[4,3,64,128]{3,2,1,0:T(8,128)(2,1)S(1)} %get-tuple-element.31), channel_id=1, source_target_pairs={{1,0},{2,1},{3,2},{4,3},{5,4},{6,5},{7,6},{8,7},{9,8},{10,9},{11,1... | collective-permute-start | bytes 589832 | tf_op jit(solution)/shard_map/ppermute | solution.py:340
  15.2 8.1 %copy-start = (s32[32]{0:T(128)S(1)}, s32[32]{0:T(128)}, u32[]{:S(2)}) copy-start(s32[32]{0:T(128)} %anchors.1) | copy-start | bytes 388
  15.2 8.1 %copy-start.1 = (s32[128]{0:T(128)S(1)}, s32[128]{0:T(128)}, u32[]{:S(2)}) copy-start(s32[128]{0:T(128)} %blocks.1) | copy-start | bytes 1540
  15.3 8.1 %copy-start.2 = (s32[128]{0:T(128)S(1)}, s32[128]{0:T(128)}, u32[]{:S(2)}) copy-start(s32[128]{0:T(128)} %param.18) | copy-start | bytes 1540
  15.3 8.1 %copy-start.3 = (f32[128]{0:T(128)S(1)}, f32[128]{0:T(128)}, u32[]{:S(2)}) copy-start(f32[128]{0:T(128)} %param.19) | copy-start | bytes 1540
  19.0 11.0 %collective-permute-start.4 = (f32[2,7,64,128]{3,2,1,0:T(8,128)S(1)}, f32[2,7,64,128]{3,2,1,0:T(8,128)S(1)}, u32[]{:S(2)}, u32[]{:S(2)}) collective-permute-start(f32[2,7,64,128]{3,2,1,0:T(8,128)S(1)} %get-tuple-element.41), channel_id=1, source_target_pairs={{0,1},{1,2},{2,3},{3,4},{4,5},{5,6},{6,7},{7,8},{8,9},{9,10},{10,1... | collective-permute-start | bytes 1376264 | tf_op jit(solution)/shard_map/ppermute | solution.py:340
  19.0 11.0 %collective-permute-start.5 = (f32[2,7,64,128]{3,2,1,0:T(8,128)S(1)}, f32[2,7,64,128]{3,2,1,0:T(8,128)S(1)}, u32[]{:S(2)}, u32[]{:S(2)}) collective-permute-start(f32[2,7,64,128]{3,2,1,0:T(8,128)S(1)} %get-tuple-element.42), channel_id=1, source_target_pairs={{1,0},{2,1},{3,2},{4,3},{5,4},{6,5},{7,6},{8,7},{9,8},{10,9},{11,1... | collective-permute-start | bytes 1376264 | tf_op jit(solution)/shard_map/ppermute | solution.py:340

commit v5 on v4

--- a/solution.py
+++ b/solution.py
@@ -1,3 +1,5 @@
+import functools
+
 import jax
 import jax.numpy as jnp
 from jax import lax
@@ -175,46 +177,38 @@
         loop(0, W - 1, take_other)
 
 
-def take_halos(fields_low, fields_high, first, second):
-    low, high = edge_scales()
-    take_fields(fields_low, low, first, second, 0, 1)
-    take_fields(fields_high, high, first, second, W + SLAB, W + SLAB)
-
-
 def inner_steps(first, second, planes, picture):
     for step in range(1, W):
         source, target = (first, second) if step % 2 else (second, first)
         advance_layers(source, target, planes, picture, W + step, W + SLAB - step)
 
 
-def outer_steps(first, second, planes, picture):
+def side_steps(high, fields, first, second, planes, picture):
+    scale = edge_scales()[high]
+    if high:
+        take_fields(fields, scale, first, second, W + SLAB, W + SLAB)
+    else:
+        take_fields(fields, scale, first, second, 0, 1)
     for step in range(1, W + 1):
         source, target = (first, second) if step % 2 else (second, first)
-        advance_layers(source, target, planes, picture, step, W + step)
-        advance_layers(source, target, planes, picture, W + SLAB - step, EXT - step)
+        low = W + SLAB - step if high else step
+        advance_layers(source, target, planes, picture, low, low + W)
 
 
 def early_kernel(
-    fields_low, media_low, fields_high, media_high, first_in, second_in, planes_in, picture_in,
-    first, second, planes, picture, up_fields, down_fields,
+    high, fields, media, first_in, second_in, planes_in, picture_in,
+    first, second, planes, picture, edge_fields,
 ):
-    low, high = edge_scales()
-
-    def halo_planes(layer):
-        store_planes(planes, layer + 1, [media_low.at[i, layer] for i in range(4)], low)
-        store_planes(planes, layer + W + SLAB, [media_high.at[i, layer] for i in range(4)], high)
-
-    loop(0, W - 1, halo_planes)
-    take_halos(fields_low, fields_high, first, second)
-    outer_steps(first, second, planes, picture)
+    scale = edge_scales()[high]
+    base = W + SLAB if high else 1
+    loop(0, W - 1, lambda layer: store_planes(planes, layer + base, [media.at[i, layer] for i in range(4)], scale))
+    side_steps(high, fields, first, second, planes, picture)
     for field in range(2):
         def pack(layer):
-            up_fields[field, layer] = first[field, layer + SLAB, BODY, :]
-            down_fields[field, layer] = first[field, layer + W, BODY, :]
+            edge_fields[field, layer] = first[field, layer + (SLAB if high else W), BODY, :]
 
         def pack_other(layer):
-            up_fields[field, layer + W] = second[field, layer + SLAB + 1, BODY, :]
-            down_fields[field, layer + W] = second[field, layer + W, BODY, :]
+            edge_fields[field, layer + W] = second[field, layer + (SLAB + 1 if high else W), BODY, :]
 
         loop(0, W, pack)
         loop(0, W - 1, pack_other)
@@ -224,12 +218,12 @@
     inner_steps(first, second, planes, picture)
 
 
-def late_kernel(
-    chosen, fields_low, fields_high, first_in, second_in, planes, picture_in,
-    first, second, picture, send,
-):
-    take_halos(fields_low, fields_high, first, second)
-    outer_steps(first, second, planes, picture)
+def late_low_kernel(fields, first_in, second_in, planes, picture_in, first, second, picture):
+    side_steps(0, fields, first, second, planes, picture)
+
+
+def late_high_kernel(chosen, fields, first_in, second_in, planes, picture_in, first, second, picture, send):
+    side_steps(1, fields, first, second, planes, picture)
     for entry in range(chosen.shape[0]):
         send[entry] = picture[pl.ds(chosen[entry], SLAB, stride=AX), :]
 
@@ -370,16 +364,21 @@
         ],
         compiler_params=grant,
     )(cur, prev, *media)
-    first, second, planes, picture, up_fields, down_fields = pl.pallas_call(
-        early_kernel,
-        out_shape=(buffer, buffer, plane, image, edge_fields, edge_fields),
-        in_specs=[VM] * 8,
-        out_specs=[VM] * 6,
-        input_output_aliases={4: 0, 5: 1, 6: 2, 7: 3},
-        compiler_params=grant,
-    )(fields_low, media_low, fields_high, media_high, first, second, planes, picture)
+    def early(high, fields, media, *state):
+        return pl.pallas_call(
+            functools.partial(early_kernel, high),
+            out_shape=(buffer, buffer, plane, image, edge_fields),
+            in_specs=[VM] * 6,
+            out_specs=[VM] * 5,
+            input_output_aliases={2: 0, 3: 1, 4: 2, 5: 3},
+            compiler_params=grant,
+        )(fields, media, *state)
+
+    *state, down_fields = early(0, fields_low, media_low, first, second, planes, picture)
+    next_high = lax.ppermute(down_fields, "depth", downward)
+    first, second, planes, picture, up_fields = early(1, fields_high, media_high, *state)
     up_fields, band_row = lax.optimization_barrier((up_fields, band_width[None, :]))
-    fields_low, fields_high = exchange(up_fields, down_fields)
+    next_low = lax.ppermute(up_fields, "depth", upward)
     chosen, place, inverse = pl.pallas_call(
         table_kernel,
         out_shape=(table, table, f32(length, length)),
@@ -396,14 +395,22 @@
         input_output_aliases={0: 0, 1: 1, 3: 2},
         compiler_params=grant,
     )(first, second, planes, picture)
+    first, second, picture = pl.pallas_call(
+        late_low_kernel,
+        out_shape=(buffer, buffer, image),
+        in_specs=[VM] * 5,
+        out_specs=[VM] * 3,
+        input_output_aliases={1: 0, 2: 1, 4: 2},
+        compiler_params=grant,
+    )(next_low, first, second, planes, picture)
     send = pl.pallas_call(
-        late_kernel,
+        late_high_kernel,
         out_shape=(buffer, buffer, image, f32(2 * shots, SLAB, AY)),
-        in_specs=[SM] + [VM] * 6,
+        in_specs=[SM] + [VM] * 5,
         out_specs=[VM] * 4,
-        input_output_aliases={3: 0, 4: 1, 6: 2},
-        compiler_params=grant,
-    )(chosen, fields_low, fields_high, first, second, planes, picture)[3]
+        input_output_aliases={2: 0, 3: 1, 5: 2},
+        compiler_params=grant,
+    )(chosen, next_high, first, second, planes, picture)[3]
     received = lax.all_to_all(send, "shot", split_axis=0, concat_axis=0, tiled=True)
     part = AY // depth
     pieces = pl.pallas_call(

time: 72.7 us -> 73.2 us (level)
    ppermute x0 -> x2, starting transfers between devices: none -> 4.32 us  [the longest x1 4.3 us: shards(): next_high = lax.ppermute(down_fields, 'depth', downward)]
    ppermute x3 -> x2, starting transfers between devices: 11.4 us -> 7.12 us  [exchange(): lax.ppermute(down, 'depth', downward)]
    all_to_all x1, blocking collectives: 17.8 us -> 19.3 us  [shards(): lax.all_to_all(pieces, 'depth', split_axis=0, concat_axis=0, tiled=True)]
    all_to_all x1, blocking collectives: 19.2 us -> 17.8 us  [shards(): lax.all_to_all(send, 'shot', split_axis=0, concat_axis=0, tiled=True)]
    pallas_call x2 -> x4, Pallas kernels: 7.39 us -> 7.82 us  [the longest x2 4.11 us: early(): pl.pallas_call(functools.partial(early_kernel, high), out_shape=(buffer,...]
    ppermute x3 -> x2, starting transfers between devices: 2.71 us -> 2.69 us  [exchange(): lax.ppermute(up, 'depth', upward)]
  transfers between devices with their start and end apart: 6 -> 6, of which waited for: 0 -> 0; matrix products, arithmetic and copies ran while one was open for 0% -> 0% of each run, Pallas kernels for 15% -> 19%
where the time goes in v5:
time: 73.2 us; the launch traced here: 73 us
  blocking collectives  37.1 us (51%)
  Pallas kernels  21.7 us (30%)
  starting transfers between devices  14.1 us (19%)
    all_to_all x1, blocking collectives, shards(): lax.all_to_all(pieces, 'depth', split_axis=0, concat_axis=0, tiled=True)  19.3 us
    all_to_all x1, blocking collectives, shards(): lax.all_to_all(send, 'shot', split_axis=0, concat_axis=0, tiled=True)  17.8 us
    ppermute x2, starting transfers between devices, exchange(): lax.ppermute(down, 'depth', downward)  7.12 us
    pallas_call x1, Pallas kernels, shards(): pl.pallas_call(table_kernel, out_shape=(table, table, f32(length, length)...  5.64 us
    ppermute x1, starting transfers between devices, shards(): next_high = lax.ppermute(down_fields, 'depth', downward)  4.3 us
    pallas_call x2, Pallas kernels, early(): pl.pallas_call(functools.partial(early_kernel, high), out_shape=(buffer,...  4.11 us
    pallas_call x1, Pallas kernels, shards(): pl.pallas_call(own_kernel, out_shape=(buffer, buffer, plane, image), in_s...  3.94 us
    ppermute x2, starting transfers between devices, exchange(): lax.ppermute(up, 'depth', upward)  2.69 us
  transfers between devices with their start and end apart: 6, of which 0 were waited for; matrix products, arithmetic and copies ran while one was open for 0% of the time, Pallas kernels for 19%

profile of v5, /device:TPU:1, one launch (start us, length us, event | category | flops | bytes accessed | tf_op | source)
XLA Modules:
  0.0 73.0 jit_solution(15631005752200453792)
XLA Ops:
  0.0 1.4 %shard_map.100 = (f32[2,7,64,128]{3,2,1,0:T(8,128)S(1)}, bf16[4,3,64,128]{3,2,1,0:T(8,128)(2,1)S(1)}, f32[2,7,64,128]{3,2,1,0:T(8,128)S(1)}, bf16[4,3,64,128]{3,2,1,0:T(8,128)(2,1)S(1)}) custom-call(f32[2,8,64,128]{3,2,1,0:T(8,128)} %bitcast.12, f32[2,8,64,128]{3,2,1,0:T(8,128)} %bitcast.14, bf16[8,64,128]{2,1,0:T(8,128)(2,1)} %bitcast.16, ...), custom_call_target="tpu_custom_call" | custom-call | tf_op jit(solution)/shard_map/pallas_call | solution.py:345
  1.4 2.7 %collective-permute-start.2 = (f32[2,7,64,128]{3,2,1,0:T(8,128)S(1)}, f32[2,7,64,128]{3,2,1,0:T(8,128)S(1)}, u32[]{:S(2)}, u32[]{:S(2)}) collective-permute-start(f32[2,7,64,128]{3,2,1,0:T(8,128)S(1)} %get-tuple-element.37), channel_id=1, source_target_pairs={{0,1},{1,2},{2,3},{3,4},{4,5},{5,6},{6,7},{7,8},{8,9},{9,10},{10,1... | collective-permute-start | bytes 1376264 | tf_op jit(solution)/shard_map/ppermute | solution.py:334
  4.1 4.2 %collective-permute-start = (f32[2,7,64,128]{3,2,1,0:T(8,128)S(1)}, f32[2,7,64,128]{3,2,1,0:T(8,128)S(1)}, u32[]{:S(2)}, u32[]{:S(2)}) collective-permute-start(f32[2,7,64,128]{3,2,1,0:T(8,128)S(1)} %get-tuple-element.35), channel_id=1, source_target_pairs={{1,0},{2,1},{3,2},{4,3},{5,4},{6,5},{7,6},{8,7},{9,8},{10,9},{11,1... | collective-permute-start | bytes 1376264 | tf_op jit(solution)/shard_map/ppermute | solution.py:334
  8.3 0.0 collective-permute-start.3
  8.3 2.9 %collective-permute-start.1 = (bf16[4,3,64,128]{3,2,1,0:T(8,128)(2,1)S(1)}, bf16[4,3,64,128]{3,2,1,0:T(8,128)(2,1)S(1)}, u32[]{:S(2)}, u32[]{:S(2)}) collective-permute-start(bf16[4,3,64,128]{3,2,1,0:T(8,128)(2,1)S(1)} %get-tuple-element.36), channel_id=1, source_target_pairs={{1,0},{2,1},{3,2},{4,3},{5,4},{6,5},{7,6},{8,7},{9,8},{10,9},{11,1... | collective-permute-start | bytes 589832 | tf_op jit(solution)/shard_map/ppermute | solution.py:334
  11.2 3.9 %shard_map.101 = (f32[2,16,80,128]{3,2,1,0:T(8,128)S(1)}, f32[2,16,80,128]{3,2,1,0:T(8,128)S(1)}, f32[10,14,64,128]{3,2,1,0:T(8,128)S(1)}, f32[512,128]{1,0:T(8,128)S(1)}) custom-call(f32[2,8,64,128]{3,2,1,0:T(8,128)} %bitcast.13, f32[2,8,64,128]{3,2,1,0:T(8,128)} %bitcast.15, bf16[8,64,128]{2,1,0:T(8,128)(2,1)} %bitcast.17, bf16[8,64,128]{2,1,0:T(8,128)(2,1)} %bitcast.19, ...), custom_call_target="tpu_custom_call" | custom-call | tf_op jit(solution)/shard_map/pallas_call | solution.py:356
  15.2 0.0 collective-permute-done.3.media
  15.2 0.0 collective-permute-done.2.fields
  15.2 2.0 %shard_map.102 = (f32[2,16,80,128]{3,2,1,0:T(8,128)S(1)}, f32[2,16,80,128]{3,2,1,0:T(8,128)S(1)}, f32[10,14,64,128]{3,2,1,0:T(8,128)S(1)}, f32[512,128]{1,0:T(8,128)S(1)}, f32[2,7,64,128]{3,2,1,0:T(8,128)S(1)}) custom-call(f32[2,7,64,128]{3,2,1,0:T(8,128)S(1)} %collective-permute-done.2.field, ...), custom_call_target="tpu_custom_call", output_to_operand_aliasing={{0}: (2, {}), {1}: (3, {}), {2}: (4, {}), {3}: (5, {})} | custom-call | tf_op jit(solution)/shard_map/pallas_call | solution.py:368
  17.3 0.0 collective-permute-done.1.media
  17.3 0.0 collective-permute-done.fields
  17.3 0.0 copy-start
  17.3 0.0 copy-start.1
  17.3 0.0 copy-start.2
  17.3 0.0 copy-start.3
  17.3 2.1 %shard_map.103 = (f32[2,16,80,128]{3,2,1,0:T(8,128)S(1)}, f32[2,16,80,128]{3,2,1,0:T(8,128)S(1)}, f32[10,14,64,128]{3,2,1,0:T(8,128)S(1)}, f32[512,128]{1,0:T(8,128)S(1)}, f32[2,7,64,128]{3,2,1,0:T(8,128)S(1)}) custom-call(f32[2,7,64,128]{3,2,1,0:T(8,128)S(1)} %collective-permute-done.fields,, ...), custom_call_target="tpu_custom_call", output_to_operand_aliasing={{0}: (2, {}), {1}: (3, {}), {2}: (4, {}), {3}: (5, {})} | custom-call | tf_op jit(solution)/shard_map/pallas_call | solution.py:368
  19.4 0.0 collective-permute-start.5
  19.4 4.3 %collective-permute-start.4 = (f32[2,7,64,128]{3,2,1,0:T(8,128)S(1)}, f32[2,7,64,128]{3,2,1,0:T(8,128)S(1)}, u32[]{:S(2)}, u32[]{:S(2)}) collective-permute-start(f32[2,7,64,128]{3,2,1,0:T(8,128)S(1)} %get-tuple-element.52), channel_id=1, source_target_pairs={{1,0},{2,1},{3,2},{4,3},{5,4},{6,5},{7,6},{8,7},{9,8},{10,9},{11,1... | collective-permute-start | bytes 1376264 | tf_op jit(solution)/shard_map/ppermute | solution.py:378
  23.7 0.0 copy-done
  23.7 0.0 copy-done.1
  23.7 0.0 copy-done.2
  23.7 0.0 copy-done.3
  23.7 5.6 %shard_map.104 = (s32[64]{0:T(128)S(1)}, s32[64]{0:T(128)S(1)}, f32[128,128]{1,0:T(8,128)S(1)}) custom-call(s32[32]{0:T(128)S(1)} %copy-done, s32[128]{0:T(128)S(1)} %copy-done.1, s32[1,128]{1,0:T(1,128)S(1)} %bitcast.10, f32[1,128]{1,0:T(1,128)S(1)} %bitcast.11), custom_call_target="tpu_custom_call" | custom-call | tf_op jit(solution)/shard_map/pallas_call | solution.py:382
  29.4 1.0 %shard_map.105 = (f32[2,16,80,128]{3,2,1,0:T(8,128)S(1)}, f32[2,16,80,128]{3,2,1,0:T(8,128)S(1)}, f32[512,128]{1,0:T(8,128)S(1)}) custom-call(f32[2,16,80,128]{3,2,1,0:T(8,128)S(1)} %get-tuple-element.54.first_in, f32[2,16,80,128]{3,2,1,0:T(8,128)S(1)} %get-tuple-element.55.second_in, ...), custom_call_target="tpu_custom_call", output_to_operand_aliasing={{0}: (0, {}), {1}: (1, {}), {2}: (3, {})} | custom-call | tf_op jit(solution)/shard_map/pallas_call | solution.py:390
  30.4 0.0 collective-permute-done.5.fields
  30.4 1.4 %shard_map.106 = (f32[2,16,80,128]{3,2,1,0:T(8,128)S(1)}, f32[2,16,80,128]{3,2,1,0:T(8,128)S(1)}, f32[512,128]{1,0:T(8,128)S(1)}) custom-call(f32[2,7,64,128]{3,2,1,0:T(8,128)S(1)} %collective-permute-done.5.fields, f32[2,16,80,128]{3,2,1,0:T(8,128)S(1)} %get-tuple-element.58.first_in, ...), custom_call_target="tpu_custom_call", output_to_operand_aliasing={{0}: (1, {}), {1}: (2, {}), {2}: (4, {})} | custom-call | tf_op jit(solution)/shard_map/pallas_call | solution.py:398
  31.9 0.0 collective-permute-done.4.fields
  31.9 2.3 %shard_map.107 = (f32[2,16,80,128]{3,2,1,0:T(8,128)S(1)}, f32[2,16,80,128]{3,2,1,0:T(8,128)S(1)}, f32[512,128]{1,0:T(8,128)S(1)}, f32[64,8,128]{2,1,0:T(8,128)S(1)}) custom-call(s32[64]{0:T(128)S(1)} %get-tuple-element.51.chosen, f32[2,7,64,128]{3,2,1,0:T(8,128)S(1)} %collective-permute-done.4.fields, ...), custom_call_target="tpu_custom_call", output_to_operand_aliasing={{0}: (2, {}), {1}: (3, {}), {2}: (5, {})} | custom-call | tf_op jit(solution)/shard_map/pallas_call | solution.py:406
  34.2 17.8 %all_to_all.10.rows_in = f32[64,8,128]{2,1,0:T(8,128)S(1)} all-to-all(f32[64,8,128]{2,1,0:T(8,128)S(1)} %get-tuple-element.64), channel_id=1, replica_groups=mesh['shot'=32,'depth'=16] {'shot'}, dimensions={0} | all-to-all | bytes 524288 | tf_op jit(solution)/shard_map/all_to_all | solution.py:414
  51.9 0.9 %shard_map.108 = f32[16,8,128]{2,1,0:T(8,128)S(1)} custom-call(s32[64]{0:T(128)S(1)} %get-tuple-element.50.place, f32[64,8,128]{2,1,0:T(8,128)S(1)} %all_to_all.10.rows_in), custom_call_target="tpu_custom_call" | custom-call | tf_op jit(solution)/shard_map/pallas_call | solution.py:416
  52.9 19.3 %all_to_all.11 = f32[16,8,128]{2,1,0:T(8,128)S(1)} all-to-all(f32[16,8,128]{2,1,0:T(8,128)S(1)} %shard_map.108), channel_id=1, replica_groups=mesh['shot'=32,'depth'=16] {'depth'}, dimensions={0} | all-to-all | bytes 131072 | tf_op jit(solution)/shard_map/all_to_all | solution.py:424
  72.2 0.9 %shard_map.109 = f32[4,8,128]{2,1,0:T(8,128)} custom-call(f32[128,128]{1,0:T(8,128)S(1)} %get-tuple-element.49.inverse, f32[128,128]{1,0:T(8,128)S(1)} %bitcast.9), custom_call_target="tpu_custom_call" | custom-call | tf_op jit(solution)/shard_map/pallas_call | solution.py:425
Async XLA Ops:
  1.4 13.8 %collective-permute-start.2 = (f32[2,7,64,128]{3,2,1,0:T(8,128)S(1)}, f32[2,7,64,128]{3,2,1,0:T(8,128)S(1)}, u32[]{:S(2)}, u32[]{:S(2)}) collective-permute-start(f32[2,7,64,128]{3,2,1,0:T(8,128)S(1)} %get-tuple-element.37), channel_id=1, source_target_pairs={{0,1},{1,2},{2,3},{3,4},{4,5},{5,6},{6,7},{7,8},{8,9},{9,10},{10,1... | collective-permute-start | bytes 1376264 | tf_op jit(solution)/shard_map/ppermute | solution.py:334
  4.1 13.2 %collective-permute-start = (f32[2,7,64,128]{3,2,1,0:T(8,128)S(1)}, f32[2,7,64,128]{3,2,1,0:T(8,128)S(1)}, u32[]{:S(2)}, u32[]{:S(2)}) collective-permute-start(f32[2,7,64,128]{3,2,1,0:T(8,128)S(1)} %get-tuple-element.35), channel_id=1, source_target_pairs={{1,0},{2,1},{3,2},{4,3},{5,4},{6,5},{7,6},{8,7},{9,8},{10,9},{11,1... | collective-permute-start | bytes 1376264 | tf_op jit(solution)/shard_map/ppermute | solution.py:334
  8.3 6.9 %collective-permute-start.3 = (bf16[4,3,64,128]{3,2,1,0:T(8,128)(2,1)S(1)}, bf16[4,3,64,128]{3,2,1,0:T(8,128)(2,1)S(1)}, u32[]{:S(2)}, u32[]{:S(2)}) collective-permute-start(bf16[4,3,64,128]{3,2,1,0:T(8,128)(2,1)S(1)} %get-tuple-element.38), channel_id=1, source_target_pairs={{0,1},{1,2},{2,3},{3,4},{4,5},{5,6},{6,7},{7,8},{8,9},{9,10},{10,1... | collective-permute-start | bytes 589832 | tf_op jit(solution)/shard_map/ppermute | solution.py:334
  8.3 9.0 %collective-permute-start.1 = (bf16[4,3,64,128]{3,2,1,0:T(8,128)(2,1)S(1)}, bf16[4,3,64,128]{3,2,1,0:T(8,128)(2,1)S(1)}, u32[]{:S(2)}, u32[]{:S(2)}) collective-permute-start(bf16[4,3,64,128]{3,2,1,0:T(8,128)(2,1)S(1)} %get-tuple-element.36), channel_id=1, source_target_pairs={{1,0},{2,1},{3,2},{4,3},{5,4},{6,5},{7,6},{8,7},{9,8},{10,9},{11,1... | collective-permute-start | bytes 589832 | tf_op jit(solution)/shard_map/ppermute | solution.py:334
  17.3 6.4 %copy-start = (s32[32]{0:T(128)S(1)}, s32[32]{0:T(128)}, u32[]{:S(2)}) copy-start(s32[32]{0:T(128)} %anchors.1) | copy-start | bytes 388
  17.3 6.4 %copy-start.1 = (s32[128]{0:T(128)S(1)}, s32[128]{0:T(128)}, u32[]{:S(2)}) copy-start(s32[128]{0:T(128)} %blocks.1) | copy-start | bytes 1540
  17.3 6.4 %copy-start.2 = (s32[128]{0:T(128)S(1)}, s32[128]{0:T(128)}, u32[]{:S(2)}) copy-start(s32[128]{0:T(128)} %param.18) | copy-start | bytes 1540
  17.3 6.4 %copy-start.3 = (f32[128]{0:T(128)S(1)}, f32[128]{0:T(128)}, u32[]{:S(2)}) copy-start(f32[128]{0:T(128)} %param.19) | copy-start | bytes 1540
  19.4 11.0 %collective-permute-start.5 = (f32[2,7,64,128]{3,2,1,0:T(8,128)S(1)}, f32[2,7,64,128]{3,2,1,0:T(8,128)S(1)}, u32[]{:S(2)}, u32[]{:S(2)}) collective-permute-start(f32[2,7,64,128]{3,2,1,0:T(8,128)S(1)} %get-tuple-element.53), channel_id=1, source_target_pairs={{0,1},{1,2},{2,3},{3,4},{4,5},{5,6},{6,7},{7,8},{8,9},{9,10},{10,1... | collective-permute-start | bytes 1376264 | tf_op jit(solution)/shard_map/ppermute | solution.py:381
  19.4 12.5 %collective-permute-start.4 = (f32[2,7,64,128]{3,2,1,0:T(8,128)S(1)}, f32[2,7,64,128]{3,2,1,0:T(8,128)S(1)}, u32[]{:S(2)}, u32[]{:S(2)}) collective-permute-start(f32[2,7,64,128]{3,2,1,0:T(8,128)S(1)} %get-tuple-element.52), channel_id=1, source_target_pairs={{1,0},{2,1},{3,2},{4,3},{5,4},{6,5},{7,6},{8,7},{9,8},{10,9},{11,1... | collective-permute-start | bytes 1376264 | tf_op jit(solution)/shard_map/ppermute | solution.py:378
